TPU v7x, 32 devices: a whole 2x2x4 slice. The times are simulated.
32 devices in a mesh: groups: 2 (over x), sp: 16 (over z, y, core).
Axes of the slice: x: 2, y: 2, z: 4, core: 2. Of those that a mesh axis runs over, the one named last changes fastest.
Arguments:
- fields: bfloat16 [2, 128, 64, 1440], P('groups', 'sp'), parts along dimension 0, may hold values from -6 to 6
- cotangent: bfloat16 [2, 128, 64, 1440], P('groups', None, 'sp'), parts along dimension 0, may hold values from -6 to 6
- ocean_mask: int32 [64, 1440], P('sp'), may hold values 0 or 1
- kernel: float32 [256, 7, 7], P('groups'), parts along dimension 0, may hold values from -0.875 to 0.875
- norm_gain: float32 [256], P('groups'), parts along dimension 0, may hold values from 0.25 to 1.75
- norm_shift: float32 [256], P('groups'), parts along dimension 0, may hold values from -3 to 3
- widen: bfloat16 [256, 256], P('groups'), parts along dimension 0, may hold values from -0.5 to 0.5
- hidden_offset: float32 [512], P('groups'), parts along dimension 0, may hold values from -3 to 3
- narrow: bfloat16 [256, 256], P('groups'), parts along dimension 0, may hold values from -0.375 to 0.375
- output_offset: float32 [256], P('groups'), parts along dimension 0, may hold values from -3 to 3
Outputs:
- updated: bfloat16 [2, 128, 64, 1440], P('groups', None, 'sp'), parts along dimension 0
- fields_grad: bfloat16 [2, 128, 64, 1440], P('groups', 'sp'), parts along dimension 0
- kernel_grad: float32 [256, 7, 7], P(('groups', 'sp')), parts along dimension 0
- widen_grad: float32 [256, 256], P(('groups', 'sp')), parts along dimension 0
- narrow_grad: float32 [256, 256], P(('groups', 'sp')), parts along dimension 0
- gain_grad: float32 [256], P('groups'), parts along dimension 0
- shift_grad: float32 [256], P('groups'), parts along dimension 0
- hidden_grad: float32 [512], P('groups'), parts along dimension 0
- output_grad: float32 [256], P('groups'), parts along dimension 0
There are 2 independent parts, one for each index of `groups`. A program takes and returns all parts, laid end to end along the dimension named above; an argument that names none is the same for every part. Nothing has to cross between parts.
Inputs may be any that keep to these rules, and one draw needn't show every extreme that they name: `ocean_mask`: 1 marks an ocean cell, 0 a land cell.
All inputs are finite; a program needn't handle non-finite values. No bound on the sum of `ocean_mask` on one device may be relied on, other than what follows from the above.
Results may differ from a plain program's by a relative error of at most 0.0064.
Values may be sent and summed in bfloat16 or wider, within the bound.
A program may use at most 128 MiB of HBM per device.

v0:
```python
import math

import jax
import jax.numpy as jnp
from jax import lax
from jax.sharding import PartitionSpec as P

KS = 7


EPSILON = 1e-06


def product(pattern, former, latter):
    return jnp.einsum(pattern, former, latter, preferred_element_type=jnp.float32)


def wrap_lon(values, rim_width):
    return jnp.concatenate([values[..., -rim_width:], values, values[..., :rim_width]], axis=-1)


def wrap_pad(values, rim_width):
    widened = wrap_lon(values, rim_width)
    return jnp.pad(widened, [(0, 0)] * (values.ndim - 2) + [(rim_width, rim_width), (0, 0)])


def apply_taps(padded, kernel_set, rows, cols):
    running = jnp.zeros(padded.shape[:2] + (rows, cols), jnp.float32)
    for row_tap in range(KS):
        for col_tap in range(KS):
            weight = kernel_set[:, row_tap, col_tap][None, :, None, None]
            running = (
                running + weight * padded[:, :, row_tap : row_tap + rows, col_tap : col_tap + cols]
            )
    return running


def tap_grads(padded, grads, rows, cols):
    return jnp.stack(
        [
            jnp.stack(
                [
                    jnp.sum(
                        padded[:, :, row_tap : row_tap + rows, col_tap : col_tap + cols] * grads,
                        axis=(0, 2, 3),
                    )
                    for col_tap in range(KS)
                ],
                axis=-1,
            )
            for row_tap in range(KS)
        ],
        axis=1,
    )


def gelu_slope(hidden):
    cdf = 0.5 * (1.0 + jax.scipy.special.erf(hidden * (1.0 / math.sqrt(2.0))))
    return cdf + hidden * jnp.exp(-0.5 * hidden * hidden) * (1.0 / math.sqrt(2.0 * math.pi))


def pointwise(conv_out, fields, cotangent, mask_rows, params):
    norm_gain, norm_shift, widen, hidden_offset, narrow, output_offset = params
    values = conv_out.astype(jnp.float32)
    centre = jnp.mean(values, axis=1, keepdims=True)
    centred = values - centre
    inv_std = lax.rsqrt(jnp.mean(centred * centred, axis=1, keepdims=True) + EPSILON)
    normed = centred * inv_std
    scaled = (normed * norm_gain[None, :, None, None] + norm_shift[None, :, None, None]).astype(
        jnp.bfloat16
    )
    hidden = product("schw,cf->sfhw", scaled, widen) + hidden_offset[None, :, None, None]
    active = jax.nn.gelu(hidden, approximate=False).astype(jnp.bfloat16)
    branch = product("sfhw,cf->schw", active, narrow) + output_offset[None, :, None, None]
    ocean_rows = mask_rows.astype(jnp.float32)[None, None]
    updated = (fields.astype(jnp.float32) + ocean_rows * branch).astype(jnp.bfloat16)
    upstream = (cotangent.astype(jnp.float32) * ocean_rows).astype(jnp.bfloat16)
    output_part = jnp.sum(upstream.astype(jnp.float32), axis=(0, 2, 3))
    narrow_part = product("schw,sfhw->cf", upstream, active)
    active_back = product("schw,cf->sfhw", upstream, narrow)
    hidden_back = (active_back * gelu_slope(hidden)).astype(jnp.bfloat16)
    hidden_part = jnp.sum(hidden_back.astype(jnp.float32), axis=(0, 2, 3))
    widen_part = product("schw,sfhw->cf", scaled, hidden_back)
    scaled_back = product("sfhw,cf->schw", hidden_back, widen)
    gain_part = jnp.sum(scaled_back * normed, axis=(0, 2, 3))
    shift_part = jnp.sum(scaled_back, axis=(0, 2, 3))
    normed_back = scaled_back * norm_gain[None, :, None, None]
    conv_back = inv_std * (
        normed_back
        - jnp.mean(normed_back, axis=1, keepdims=True)
        - normed * jnp.mean(normed_back * normed, axis=1, keepdims=True)
    )
    return (
        updated,
        conv_back.astype(jnp.bfloat16),
        (widen_part, narrow_part, gain_part, shift_part, hidden_part, output_part),
    )


def local(
    fields,
    cotangent,
    ocean_mask,
    kernel,
    norm_gain,
    norm_shift,
    widen,
    hidden_offset,
    narrow,
    output_offset,
):
    params = (norm_gain, norm_shift, widen, hidden_offset, narrow, output_offset)
    rim_width = KS // 2
    local_rows = cotangent.shape[2]
    local_channels = fields.shape[1]
    lat_all = local_rows * lax.axis_size("sp")
    lon_cells = fields.shape[3]
    grad_scale = 1.0 / math.sqrt(fields.shape[0] * lat_all * lon_cells)
    own_kernel = lax.dynamic_slice_in_dim(
        kernel, lax.axis_index("sp") * local_channels, local_channels, 0
    )
    padded = wrap_pad(fields.astype(jnp.float32), rim_width)
    conv_out = apply_taps(padded, own_kernel, lat_all, lon_cells).astype(jnp.bfloat16)
    conv_rows, field_rows = (
        lax.all_to_all(conv_out, "sp", split_axis=2, concat_axis=1, tiled=True),
        lax.all_to_all(fields, "sp", split_axis=2, concat_axis=1, tiled=True),
    )
    updated, conv_back, partials = pointwise(conv_rows, field_rows, cotangent, ocean_mask, params)
    back_cols, upstream_cols = (
        lax.all_to_all(conv_back, "sp", split_axis=1, concat_axis=2, tiled=True),
        lax.all_to_all(cotangent, "sp", split_axis=1, concat_axis=2, tiled=True),
    )
    back_values = back_cols.astype(jnp.float32)
    kernel_grad = tap_grads(padded, back_values, lat_all, lon_cells) * grad_scale
    spread = apply_taps(
        wrap_pad(back_values, rim_width), own_kernel[:, ::-1, ::-1], lat_all, lon_cells
    )
    fields_grad = (upstream_cols.astype(jnp.float32) + spread).astype(jnp.bfloat16)
    widen_part, narrow_part, gain_part, shift_part, hidden_part, output_part = partials
    widen_sum, narrow_sum = (
        lax.psum_scatter(widen_part, "sp", scatter_dimension=0, tiled=True),
        lax.psum_scatter(narrow_part, "sp", scatter_dimension=0, tiled=True),
    )
    gain_sum, shift_sum, hidden_sum, output_sum = lax.psum(
        (gain_part, shift_part, hidden_part, output_part), "sp"
    )
    return (
        updated,
        fields_grad,
        kernel_grad,
        widen_sum * grad_scale,
        narrow_sum * grad_scale,
        gain_sum * grad_scale,
        shift_sum * grad_scale,
        hidden_sum * grad_scale,
        output_sum * grad_scale,
    )


def solution(mesh):
    return jax.shard_map(
        local,
        mesh=mesh,
        in_specs=(
            P("groups", "sp", None, None),
            P("groups", None, "sp", None),
            P("sp", None),
            P("groups", None, None),
            P("groups"),
            P("groups"),
            P("groups", None),
            P("groups"),
            P("groups", None),
            P("groups"),
        ),
        out_specs=(
            P("groups", None, "sp", None),
            P("groups", "sp", None, None),
            P(("groups", "sp"), None, None),
            P(("groups", "sp"), None),
            P(("groups", "sp"), None),
            P("groups"),
            P("groups"),
            P("groups"),
            P("groups"),
        ),
        check_vma=False,
    )
```

profile of v0, /device:TPU:0, one launch (start us, length us, event | category | flops | bytes accessed | tf_op | source)
XLA Modules:
  0.0 433.4 jit_solution(14692264688209789156)
XLA Ops:
  7.2 2.4 copy_convert_fusion
  9.6 1.7 copy-done.3
  11.2 0.8 fusion.120
  12.0 3.6 concatenate.26
  15.6 1.1 fusion.107
  17.6 41.0 %fusion.85 = bf16[1,8,64,1440]{3,1,0,2:T(8,128)(2,1)} fusion(f32[8]{0:T(128)} %get-tuple-element.138, f32[8]{0:T(128)S(1)} %get-tuple-element.91, f32[8]{0:T(128)S(1)} %get-tuple-element.92, f32[8]{0:T(128)S(1)} %get-tuple-element.93, f32[8]{0:T(128)S(1)} %get-tuple-element.94, f32[8]{0:T(128)S(1)} %get-tuple-element.95, f32[8]{0:T(128)S(1)} %get-tuple-element.96, ...), kind=kLoop, calls=%fused_computation.181 | loop fusion | flops 76677120 | bytes 7398944 | tf_op jit(solution)/shard_map/convert_element_type | solution.py:123
  58.6 7.5 %all-to-all-start.1 = ((bf16[1,8,64,1440]{3,1,0,2:T(8,128)(2,1)}), bf16[1,8,64,1440]{3,1,0,2:T(8,128)(2,1)S(1)}, u32[]{:S(2)}, u32[]{:S(2)}) async-start(bf16[1,8,64,1440]{3,1,0,2:T(8,128)(2,1)} %fusion.85), calls=%async_computation.1 | async-start | bytes 3145728 | tf_op jit(solution)/shard_map/all_to_all | solution.py:125
  66.2 3.5 copy.62
  69.9 2.7 copy.69
  72.6 1.5 convert_reduce_fusion.1
  74.1 24.1 %all-to-all-done.1 = bf16[1,8,64,1440]{3,1,0,2:T(8,128)(2,1)S(1)} async-done(((bf16[1,8,64,1440]{3,1,0,2:T(8,128)(2,1)}), bf16[1,8,64,1440]{3,1,0,2:T(8,128)(2,1)S(1)}, u32[]{:S(2)}, u32[]{:S(2)}) %all-to-all-start.1) | async-done | bytes 1474592 | tf_op jit(solution)/shard_map/all_to_all | solution.py:125
  98.1 9.3 %all-to-all-start.2 = ((bf16[1,128,4,1440]{3,2,0,1:T(4,128)(2,1)}), bf16[1,128,4,1440]{3,2,0,1:T(4,128)(2,1)}, u32[]{:S(2)}, u32[]{:S(2)}) async-start(bf16[1,128,4,1440]{3,2,0,1:T(4,128)(2,1)} %copy.69), calls=%async_computation.2 | async-start | bytes 3145728 | tf_op jit(solution)/shard_map/all_to_all | solution.py:131
  107.8 2.0 copy_bitcast_fusion.1
  110.3 2.4 copy.67
  112.7 16.3 %fusion.2 = (bf16[256,4,1440]{0,2,1:T(8,128)(2,1)}, f32[4,1440,256]{2,1,0:T(8,128)}) fusion(f32[256]{0:T(256)S(1)} %copy-done.79, bf16[128,256]{1,0:T(8,128)(2,1)S(1)} %copy-done, f32[128,4,1440]{0,2,1:T(8,128)S(1)} %copy.67, f32[128]{0:T(128)S(1)} %copy-done.78, f32[128]{0:T(128)S(1)} %copy-done.73, f32[4,1440]{1,0:T(4,128)S(1)} %add_rsqrt_fusion, ...), kind=kOutput, calls=%fused_computation.4 | convolution fusion | flops 478494720 | bytes 11910144 | tf_op jit(solution)/shard_map/schw,cf->sfhw/dot_general | solution.py:15
  129.0 10.5 %all-to-all-done.2 = bf16[1,128,4,1440]{3,2,0,1:T(4,128)(2,1)} async-done(((bf16[1,128,4,1440]{3,2,0,1:T(4,128)(2,1)}), bf16[1,128,4,1440]{3,2,0,1:T(4,128)(2,1)}, u32[]{:S(2)}, u32[]{:S(2)}) %all-to-all-start.2) | async-done | bytes 1474592 | tf_op jit(solution)/shard_map/all_to_all | solution.py:131
  139.5 9.1 %all-to-all-start = ((bf16[1,8,64,1440]{3,1,0,2:T(8,128)(2,1)}), bf16[1,8,64,1440]{3,1,0,2:T(8,128)(2,1)}, u32[]{:S(2)}, u32[]{:S(2)}) async-start(bf16[1,8,64,1440]{3,1,0,2:T(8,128)(2,1)} %copy.62), calls=%async_computation | async-start | bytes 3145728 | tf_op jit(solution)/shard_map/all_to_all | solution.py:126
  148.7 6.5 %convert_reduce_fusion = (f32[256]{0:T(256)}, bf16[256,4,1440]{0,2,1:T(8,128)(2,1)S(1)}) fusion(f32[4,1440,256]{2,1,0:T(8,128)} %get-tuple-element.140, f32[256]{0:T(256)S(1)} %copy-done.79, bf16[128,256]{1,0:T(8,128)(2,1)S(1)} %copy-done.12, f32[4,1440]{1,0:T(4,128)S(1)} %convert_element_type.145, bf16[1,128,4,1440]{1,3,2,0:T(8,128)(2,1)} %param.11), kind=kOutput, calls=%fused_computation.18 | convolution fusion | flops 398868224 | bytes 10412544 | tf_op jit(solution)/shard_map/schw,cf->sfhw/dot_general | solution.py:15
  155.2 1.6 copy-done.11
  156.8 1.6 fusion.98
  158.4 5.3 %fusion.75 = (f32[128]{0:T(128)S(1)}, f32[4,1440]{1,0:T(4,128)S(1)}, f32[4,1440]{1,0:T(4,128)S(1)}, f32[4,1440,128]{2,1,0:T(8,128)}) fusion(f32[128,4,1440]{0,2,1:T(8,128)S(1)} %copy.67, f32[4,1440]{1,0:T(4,128)S(1)} %add_rsqrt_fusion, f32[4,1440]{1,0:T(4,128)S(1)} %broadcast_multiply_fusion.3, f32[128]{0:T(128)S(1)} %copy-done.74, ...), kind=kOutput, calls=%fused_computation.164 | convolution fusion | flops 383373952 | bytes 9006080 | tf_op jit(solution)/shard_map/sfhw,cf->schw/dot_general | solution.py:15
  163.7 2.6 reduce_sum.567
  166.4 8.0 %fusion.87 = bf16[1,128,4,1440]{1,3,2,0:T(8,128)(2,1)} fusion(f32[128,4,1440]{0,2,1:T(8,128)S(1)} %copy.67, f32[4,1440,128]{2,1,0:T(8,128)} %get-tuple-element.141, f32[4,1440]{1,0:T(4,128)S(1)} %get-tuple-element.144, f32[4,1440]{1,0:T(4,128)S(1)} %get-tuple-element.145, f32[128]{0:T(128)S(1)} %copy-done.74, f32[4,1440]{1,0:T(4,128)S(1)} %add_rsqrt_fusion, ...), kind=kLoop, calls=%fused_computation.183 | loop fusion | flops 5898240 | bytes 7465472 | tf_op jit(solution)/shard_map/convert_element_type | solution.py:95
  174.3 3.9 copy.72
  178.2 2.5 all-to-all-done
  180.7 9.1 %all-to-all-start.3 = ((bf16[1,128,4,1440]{3,2,0,1:T(4,128)(2,1)}), bf16[1,128,4,1440]{3,2,0,1:T(4,128)(2,1)S(1)}, u32[]{:S(2)}, u32[]{:S(2)}) async-start(bf16[1,128,4,1440]{3,2,0,1:T(4,128)(2,1)} %copy.72), calls=%async_computation.3 | async-start | bytes 3145728 | tf_op jit(solution)/shard_map/all_to_all | solution.py:130
  189.9 1.9 convert_bitcast_fusion.1
  191.7 1.8 copy.71
  193.6 3.5 copy_bitcast_fusion
  197.1 3.6 copy.68
  200.7 4.1 fusion.95
  204.9 39.0 %all-reduce.2 = (f32[128]{0:T(128)S(1)}, f32[128]{0:T(128)S(1)}, f32[256]{0:T(256)S(1)}, f32[128]{0:T(128)S(1)}) all-reduce(f32[128]{0:T(128)S(1)} %get-tuple-element.78, f32[128]{0:T(128)S(1)} %reduce_sum.567, f32[256]{0:T(256)S(1)} %copy-done.76, f32[128]{0:T(128)S(1)} %copy-done.75), channel_id=1, replica_groups=mesh['groups'=2,'sp'=16] {'sp'}, use_global_device_ids=true, to_apply=%region_56.57 | all-reduce | flops 640 | bytes 5120 | tf_op jit(solution)/shard_map/psum | solution.py:144
  245.5 4.8 %fusion.76 = bf16[1,128,4,1440]{1,3,2,0:T(8,128)(2,1)} fusion(f32[128,4,1440]{0,2,1:T(8,128)} %copy.68, bf16[256,4,1440]{0,2,1:T(8,128)(2,1)} %get-tuple-element.139, f32[128]{0:T(128)S(1)} %copy-done.77, f32[4,1440]{1,0:T(4,128)S(1)} %convert_element_type.145, bf16[128,256]{1,0:T(8,128)(2,1)S(1)} %copy-done.12), kind=kOutput, calls=%fused_computation.171 | convolution fusion | flops 380436480 | bytes 7461888 | tf_op jit(solution)/shard_map/sfhw,cf->schw/dot_general | solution.py:15
  250.3 1.3 broadcast_multiply_fusion.5
  251.6 34.1 %reduce-scatter.5.cloned.1.call-done = f32[8,256]{1,0:T(8,128)} async-done(((f32[128,256]{1,0:T(8,128)}), f32[8,256]{1,0:T(8,128)}) %reduce-scatter.5.cloned.1.call-update) | async-done | bytes 8208 | tf_op jit(solution)/shard_map/reduce_scatter | solution.py:142
  285.7 1.3 broadcast_multiply_fusion.4
  287.7 1.6 copy-done.2
  289.3 14.9 %multiply_reduce_fusion = (f32[8]{0:T(128)S(1)}, f32[8]{0:T(128)S(1)}, f32[8]{0:T(128)}, f32[8]{0:T(128)}, f32[8]{0:T(128)}, /*index=5*/f32[8]{0:T(128)}, f32[8]...) fusion(f32[1,8,64,1440]{3,1,2,0:T(8,128)S(1)} %bitcast.310, ...), kind=kLoop, calls=%fused_computation.98 | loop fusion | flops 26541936 | bytes 5911104 | tf_op jit(solution)/shard_map/reduce_sum | solution.py:43
  304.2 14.2 %multiply_reduce_fusion.1 = (f32[8]{0:T(128)}, f32[8]{0:T(128)}, f32[8]{0:T(128)}, f32[8]{0:T(128)}, f32[8]{0:T(128)}, /*index=5*/f32[8]{0:T(128)}, f32[8]{0:T(1...) fusion(f32[1,8,64,1440]{3,1,2,0:T(8,128)S(1)} %bitcast.311, ...), kind=kLoop, calls=%fused_computation.99 | loop fusion | flops 26541936 | bytes 5911104 | tf_op jit(solution)/shard_map/reduce_sum | solution.py:43
  318.4 8.7 %multiply_reduce_fusion.21 = (f32[8]{0:T(128)S(1)}, f32[8]{0:T(128)S(1)}, f32[8]{0:T(128)S(1)}, f32[8]{0:T(128)S(1)}, f32[8]{0:T(128)S(1)}, /*index=5*/f32[8]{0:T(128)S(1)}, f32[8]{0:T(128)S(1)}) fusion(f32[1,8,64,1440]{3,1,2,0:T(8,128)S(1)} %bitcast.312, f32[1,8,64,3]{3,1,2,0:T(8,128)S(1)} %copy-done.10, f32[1,8,64,1440]{3,1,2,0:T(8,128)S(1)} %copy-done.4, ...), kind=kLoop, calls=%fused_computation.119 | loop fusion | flops 15482824 | bytes 7385312 | tf_op jit(solution)/shard_map/reduce_sum | solution.py:43
  327.2 4.4 %multiply_reduce_fusion.43 = (f32[8]{0:T(128)S(1)}, f32[8]{0:T(128)S(1)}, f32[8]{0:T(128)S(1)}, f32[8]{0:T(128)S(1)}, f32[8]{0:T(128)S(1)}, /*index=5*/f32[8]{0:T(128)S(1)}) fusion(f32[1,8,64,1440]{3,1,2,0:T(8,128)S(1)} %bitcast.313, f32[1,8,64,1446]{3,1,2,0:T(8,128)S(1)} %copy-done.2), kind=kLoop, calls=%fused_computation.141 | loop fusion | flops 8847312 | bytes 5910720 | tf_op jit(solution)/shard_map/reduce_sum | solution.py:43
  331.6 0.8 fusion.119
  334.0 0.7 stack.235
  334.9 0.7 stack.217
  335.7 0.7 stack.208
  337.4 4.0 concatenate.29
  341.6 83.0 %add_convert_fusion.1 = bf16[1,8,64,1440]{3,1,2,0:T(8,128)(2,1)S(1)} fusion(f32[1,8,64,1440]{3,1,2,0:T(8,128)} %bitcast.321, f32[1,8,64,1446]{3,1,2,0:T(8,128)} %concatenate.29, f32[1,8,64,3]{3,1,2,0:T(8,128)S(1)} %get-tuple-element.86, f32[1,8,64,1440]{3,1,2,0:T(8,128)S(1)} %bitcast.316, f32[1,8,64,3]{3,1,2,0:T(8,128)} %get-tuple-element.87, ...), kind=kLoop, calls=%fused_computation.147 | loop fusion | flops 77414400 | bytes 10348064 | tf_op jit(solution)/shard_map/convert_element_type | solution.py:138
  424.6 1.6 copy.83
  (195 shorter events, 6.7 us)
Async XLA Ops:
  7.2 105.5 %copy-start = (bf16[128,256]{1,0:T(8,128)(2,1)S(1)}, bf16[128,256]{1,0:T(8,128)(2,1)}, u32[]{:S(2)}) copy-start(bf16[128,256]{1,0:T(8,128)(2,1)} %param.16) | copy-start | bytes 196612
  9.6 1.7 copy-start.3
  12.0 3.6 copy-start.14
  15.6 43.0 %copy-start.1 = (f32[1,8,64,1446]{3,1,2,0:T(8,128)}, f32[1,8,64,1446]{3,1,2,0:T(8,128)S(1)}, u32[]{:S(2)}) copy-start(f32[1,8,64,1446]{3,1,2,0:T(8,128)S(1)} %concatenate.26) | copy-start | bytes 8884228
  58.6 11.1 %copy-start.13 = (s32[4,1440]{1,0:T(4,128)S(1)}, s32[4,1440]{1,0:T(4,128)}, u32[]{:S(2)}) copy-start(s32[4,1440]{1,0:T(4,128)} %param.12) | copy-start | bytes 69124
  58.6 11.1 %copy-start.78 = (f32[128]{0:T(128)S(1)}, f32[128]{0:T(128)}, u32[]{:S(2)}) copy-start(f32[128]{0:T(128)} %param.15) | copy-start | bytes 1540
  58.6 11.2 %copy-start.73 = (f32[128]{0:T(128)S(1)}, f32[128]{0:T(128)}, u32[]{:S(2)}) copy-start(f32[128]{0:T(128)} %param.14) | copy-start | bytes 1540
  58.6 39.5 %all-to-all-start.1 = ((bf16[1,8,64,1440]{3,1,0,2:T(8,128)(2,1)}), bf16[1,8,64,1440]{3,1,0,2:T(8,128)(2,1)S(1)}, u32[]{:S(2)}, u32[]{:S(2)}) async-start(bf16[1,8,64,1440]{3,1,0,2:T(8,128)(2,1)} %fusion.85), calls=%async_computation.1 | async-start | bytes 3145728 | tf_op jit(solution)/shard_map/all_to_all | solution.py:125
  66.2 3.7 copy-start.8
  98.1 11.7 %copy-start.5 = (bf16[1,8,64,1440]{3,1,0,2:T(8,128)(2,1)}, bf16[1,8,64,1440]{3,1,0,2:T(8,128)(2,1)S(1)}, u32[]{:S(2)}) copy-start(bf16[1,8,64,1440]{3,1,0,2:T(8,128)(2,1)S(1)} %all-to-all-done.1) | copy-start | bytes 4423684
  98.1 41.4 %all-to-all-start.2 = ((bf16[1,128,4,1440]{3,2,0,1:T(4,128)(2,1)}), bf16[1,128,4,1440]{3,2,0,1:T(4,128)(2,1)}, u32[]{:S(2)}, u32[]{:S(2)}) async-start(bf16[1,128,4,1440]{3,2,0,1:T(4,128)(2,1)} %copy.69), calls=%async_computation.2 | async-start | bytes 3145728 | tf_op jit(solution)/shard_map/all_to_all | solution.py:131
  110.3 2.4 copy-start.79
  129.0 19.7 %copy-start.12 = (bf16[128,256]{1,0:T(8,128)(2,1)S(1)}, bf16[128,256]{1,0:T(8,128)(2,1)}, u32[]{:S(2)}) copy-start(bf16[128,256]{1,0:T(8,128)(2,1)} %param.18) | copy-start | bytes 196612
  139.5 41.2 %all-to-all-start = ((bf16[1,8,64,1440]{3,1,0,2:T(8,128)(2,1)}), bf16[1,8,64,1440]{3,1,0,2:T(8,128)(2,1)}, u32[]{:S(2)}, u32[]{:S(2)}) async-start(bf16[1,8,64,1440]{3,1,0,2:T(8,128)(2,1)} %copy.62), calls=%async_computation | async-start | bytes 3145728 | tf_op jit(solution)/shard_map/all_to_all | solution.py:126
  148.7 101.7 %reduce-scatter.3.cloned.1.call-start = ((), (), s32[]{:S(2)}) async-start(), calls=%async_computation.6 | async-start | bytes 139264 | tf_op jit(solution)/shard_map/reduce_scatter | solution.py:141
  148.7 8.1 %copy-start.6 = (bf16[1,8,64,1440]{3,1,0,2:T(8,128)(2,1)S(1)}, bf16[1,8,64,1440]{3,1,0,2:T(8,128)(2,1)}, u32[]{:S(2)}) copy-start(bf16[1,8,64,1440]{3,1,0,2:T(8,128)(2,1)} %copy-done.5) | copy-start | bytes 4423684
  155.2 1.6 copy-start.11
  156.8 1.6 copy-start.74
  180.7 106.3 %all-to-all-start.3 = ((bf16[1,128,4,1440]{3,2,0,1:T(4,128)(2,1)}), bf16[1,128,4,1440]{3,2,0,1:T(4,128)(2,1)S(1)}, u32[]{:S(2)}, u32[]{:S(2)}) async-start(bf16[1,128,4,1440]{3,2,0,1:T(4,128)(2,1)} %copy.72), calls=%async_computation.3 | async-start | bytes 3145728 | tf_op jit(solution)/shard_map/all_to_all | solution.py:130
  189.8 95.9 %reduce-scatter.5.cloned.1.call-start = ((), (), s32[]{:S(2)}) async-start(), calls=%async_computation.7 | async-start | bytes 139264 | tf_op jit(solution)/shard_map/reduce_scatter | solution.py:142
  197.1 3.6 copy-start.9
  200.7 4.2 copy-start.75
  200.7 4.2 copy-start.76
  200.7 44.8 %copy-start.77 = (f32[128]{0:T(128)S(1)}, f32[128]{0:T(128)}, u32[]{:S(2)}) copy-start(f32[128]{0:T(128)} %param.19) | copy-start | bytes 1540
  287.4 1.9 copy-start.2
  304.2 14.2 %copy-start.4 = (f32[1,8,64,1440]{3,1,2,0:T(8,128)S(1)}, f32[1,8,64,1440]{3,1,2,0:T(8,128)}, u32[]{:S(2)}) copy-start(f32[1,8,64,1440]{3,1,2,0:T(8,128)} %copy-done.3) | copy-start | bytes 8847364
  304.2 14.2 %copy-start.7 = (bf16[1,8,64,1440]{3,2,1,0:T(8,128)(2,1)S(1)}, bf16[1,8,64,1440]{3,2,1,0:T(8,128)(2,1)}, u32[]{:S(2)}) copy-start(bf16[1,8,64,1440]{3,2,1,0:T(8,128)(2,1)} %param.10) | copy-start | bytes 4423684
  304.2 14.2 %copy-start.10 = (f32[1,8,64,3]{3,1,2,0:T(8,128)S(1)}, f32[1,8,64,3]{3,1,2,0:T(8,128)}, u32[]{:S(2)}) copy-start(f32[1,8,64,3]{3,1,2,0:T(8,128)} %get-tuple-element.89) | copy-start | bytes 18436
  337.2 4.2 copy-start.16
  337.2 4.2 copy-start.18
  337.2 4.2 copy-start.20
  337.2 4.2 copy-start.22
  337.2 4.2 copy-start.24
  337.2 4.2 copy-start.26
  337.2 4.2 copy-start.28
  337.3 4.2 copy-start.30
  337.3 4.2 copy-start.32
  337.3 4.2 copy-start.34
  337.3 4.2 copy-start.36
  337.3 4.2 copy-start.38
  337.3 4.2 copy-start.40
  337.3 4.2 copy-start.42
  337.3 4.2 copy-start.44
  337.3 4.2 copy-start.46
  337.3 4.2 copy-start.48
  337.4 4.2 copy-start.50
  337.4 4.2 copy-start.52
  337.4 4.2 copy-start.54
  (38 other events, 21.8 us)
Sparse Core Ops, SparseCore 0:
  158.6 68.8 reduce-scatter.2
  231.5 54.1 reduce-scatter.4
where the time goes:
time: 442 us; the launch traced here: 433 us
  other arithmetic  194 us (44%)
  waiting for transfers between devices  71.1 us (16%)
  local copies, waits for them, and re-layouts  40 us (9%)
  blocking collectives  39 us (9%)
  matrix products  38.6 us (9%)
  starting transfers between devices  35.2 us (8%)
  between operations  15.5 us (4%)
    convert_element_type x1, other arithmetic, local(): (upstream_cols.astype(jnp.float32) + spread).astype(jnp.bfloat16)  83 us
    reduce_sum x4, other arithmetic, tap_grads(): jnp.sum(padded[:, :, row_tap:row_tap + rows, col_tap:col_tap + cols] * gr...  42.2 us
    convert_element_type x1, other arithmetic, local(): apply_taps(padded, own_kernel, lat_all, lon_cells).astype(jnp.bfloat16)  41 us
    psum x1, blocking collectives, local(): lax.psum((gain_part, shift_part, hidden_part, output_part), 'sp')  39 us
    dot_general x6, matrix products, product(): jnp.einsum(pattern, former, latter, preferred_element_type=jnp.float32)  38.6 us
    reduce_scatter x1, waiting for transfers between devices, local(): lax.psum_scatter(narrow_part, 'sp', scatter_dimension=0, tiled=True)  34.1 us
    all_to_all x1, waiting for transfers between devices, local(): lax.all_to_all(conv_out, 'sp', split_axis=2, concat_axis=1, tiled=True)  24.1 us
    unnamed x169, local copies, waits for them, and re-layouts  13.4 us
  transfers between devices with their start and end apart: 6, of which 4 were waited for; matrix products, arithmetic and copies ran while one was open for 19% of the time, Pallas kernels for 0%

commit v1 on v0

v1 whole, which is shorter than its diff:
```python
import functools
import math

import jax
import jax.numpy as jnp
import numpy as np
from jax import lax
from jax.experimental import pallas as pl
from jax.experimental.pallas import tpu as pltpu
from jax.sharding import PartitionSpec as P

KS = 7
RIM = KS // 2
EPSILON = 1e-06
GROUP = 16
NT = (((1,), (1,)), ((), ()))


def dot(former, latter):
    return jnp.dot(former, latter, preferred_element_type=jnp.float32)


def dot_nt(former, latter):
    return lax.dot_general(former, latter, NT, preferred_element_type=jnp.float32)


def band_matrix(kernel, rows):
    channels = kernel.shape[0]
    taps = jnp.swapaxes(kernel, 1, 2)
    shifted = jnp.stack([jnp.pad(taps, ((0, 0), (0, 0), (h, rows - 1 - h))) for h in range(rows)])
    span = KS * (rows + KS - 1)
    shifted = shifted.reshape(rows, channels, span).astype(jnp.bfloat16)
    spread = jnp.asarray(np.repeat(np.eye(span, dtype=np.float32), GROUP, axis=1), jnp.bfloat16)
    wide = jnp.einsum("hck,kn->hcn", shifted, spread, preferred_element_type=jnp.float32)
    same = (jnp.arange(channels)[:, None] % GROUP) == (jnp.arange(span * GROUP)[None, :] % GROUP)
    return jnp.where(same[None], wide, 0.0).astype(jnp.bfloat16)


def shifts(values, scratch):
    rows, group, lon = values.shape
    flat = values.reshape(rows * group, lon)
    wrapped = jnp.concatenate([flat[:, -RIM:], flat, flat[:, :RIM]], axis=1)
    for tap in range(KS):
        scratch[tap * rows * group : (tap + 1) * rows * group, :] = wrapped[:, tap : tap + lon]


def conv_kernel(above, own, below, band, out, scratch):
    rows, group, lon = own.shape
    shifts(jnp.concatenate([above[...], own[...], below[...]], axis=0), scratch)
    result = dot(band[...].reshape(rows * group, -1), scratch[...])
    out[...] = result.astype(out.dtype).reshape(rows, group, lon)


def back_kernel(x_above, x_own, x_below, g_above, g_own, g_below, cotangent, band, out, parts, scratch):
    rows, group, lon = x_own.shape
    grads = g_own[...].reshape(rows * group, lon)
    shifts(jnp.concatenate([x_above[...], x_own[...], x_below[...]], axis=0), scratch)
    pairs = dot_nt(grads, scratch[...])
    row = lax.broadcasted_iota(jnp.int32, pairs.shape, 0) % group
    col = lax.broadcasted_iota(jnp.int32, pairs.shape, 1) % group
    kept = jnp.where(row == col, pairs, 0.0)
    parts[...] = jnp.sum(kept.reshape(rows, group, -1), axis=1)[None]
    shifts(jnp.concatenate([g_above[...], g_own[...], g_below[...]], axis=0), scratch)
    spread = dot(band[...].reshape(rows * group, -1), scratch[...])
    total = cotangent[...].reshape(rows * group, lon).astype(jnp.float32) + spread
    out[...] = total.astype(out.dtype).reshape(rows, group, lon)


def pointwise_kernel(
    conv, fields, cotangent, mask, gain, shift, widen, widen_t, hidden_off, narrow, narrow_t, out_off,
    updated, conv_back, widen_part, narrow_part, gain_part, shift_part, hidden_part, out_part,
):
    lon = conv.shape[-1]

    @pl.when(pl.program_id(0) == 0)
    def _():
        for part in (widen_part, narrow_part, gain_part, shift_part, hidden_part, out_part):
            part[...] = jnp.zeros_like(part)

    f32, bf16 = jnp.float32, jnp.bfloat16
    step = 256
    for first in range(0, lon, step):
        cols = slice(first, min(first + step, lon))
        values = conv[0, :, cols].astype(f32)
        centre = jnp.mean(values, axis=0, keepdims=True)
        centred = values - centre
        inv_std = lax.rsqrt(jnp.mean(centred * centred, axis=0, keepdims=True) + EPSILON)
        normed = centred * inv_std
        scaled = (normed * gain[...] + shift[...]).astype(bf16)
        hidden = dot(widen_t[...], scaled) + hidden_off[...]
        cdf = 0.5 * (1.0 + lax.erf(hidden * (1.0 / math.sqrt(2.0))))
        active = (hidden * cdf).astype(bf16)
        slope = cdf + hidden * jnp.exp(-0.5 * hidden * hidden) * (1.0 / math.sqrt(2.0 * math.pi))
        ocean = mask[0, :, cols].astype(f32)
        branch = dot(narrow[...], active) + out_off[...]
        updated[0, :, cols] = (fields[0, :, cols].astype(f32) + ocean * branch).astype(bf16)
        upstream_wide = cotangent[0, :, cols].astype(f32) * ocean
        upstream = upstream_wide.astype(bf16)
        out_part[...] += jnp.sum(upstream_wide, axis=1, keepdims=True)
        narrow_part[...] += dot_nt(upstream, active)
        hidden_wide = dot(narrow_t[...], upstream) * slope
        hidden_back = hidden_wide.astype(bf16)
        hidden_part[...] += jnp.sum(hidden_wide, axis=1, keepdims=True)
        widen_part[...] += dot_nt(scaled, hidden_back)
        scaled_back = dot(widen[...], hidden_back)
        gain_part[...] += jnp.sum(scaled_back * normed, axis=1, keepdims=True)
        shift_part[...] += jnp.sum(scaled_back, axis=1, keepdims=True)
        normed_back = scaled_back * gain[...]
        conv_back[0, :, cols] = (
            inv_std
            * (
                normed_back
                - jnp.mean(normed_back, axis=0, keepdims=True)
                - normed * jnp.mean(normed_back * normed, axis=0, keepdims=True)
            )
        ).astype(bf16)


def halos(values, devices):
    above = lax.ppermute(values[-RIM:], "sp", [(d, d + 1) for d in range(devices - 1)])
    below = lax.ppermute(values[:RIM], "sp", [(d + 1, d) for d in range(devices - 1)])
    return above, below


def local(
    fields, cotangent, ocean_mask, kernel, norm_gain, norm_shift, widen, hidden_offset, narrow, output_offset
):
    devices = lax.axis_size("sp")
    samples, channels, rows, lon = cotangent.shape
    wide = widen.shape[1]
    f32, bf16 = jnp.float32, jnp.bfloat16
    grad_scale = 1.0 / math.sqrt(samples * rows * devices * lon)
    groups = channels // GROUP
    span = KS * (rows + KS - 1) * GROUP
    params = pltpu.CompilerParams(vmem_limit_bytes=48 * 1024 * 1024)

    band = band_matrix(kernel, rows)
    band_back = band_matrix(kernel[:, ::-1, ::-1], rows)
    cot_rows = jnp.swapaxes(cotangent[0], 0, 1)

    own = lax.all_to_all(fields, "sp", split_axis=2, concat_axis=1, tiled=True)
    own = jnp.swapaxes(own[0], 0, 1)
    above, below = halos(own, devices)

    def rows_spec(count):
        return pl.BlockSpec((count, GROUP, lon), lambda g: (0, g, 0))

    band_spec = pl.BlockSpec((rows, GROUP, span), lambda g: (0, g, 0))
    conv_out = pl.pallas_call(
        conv_kernel,
        name="depthwise",
        grid=(groups,),
        in_specs=[rows_spec(RIM), rows_spec(rows), rows_spec(RIM), band_spec],
        out_specs=rows_spec(rows),
        out_shape=jax.ShapeDtypeStruct((rows, channels, lon), bf16),
        scratch_shapes=[pltpu.VMEM((span, lon), bf16)],
        compiler_params=params,
    )(above, own, below, band)

    def row_spec(count):
        return pl.BlockSpec((1, count, lon), lambda h: (h, 0, 0))

    def whole(*shape):
        return pl.BlockSpec(shape, lambda h: (0,) * len(shape))

    column = lambda vector: vector[:, None]
    updated, conv_back, widen_part, narrow_part, gain_part, shift_part, hidden_part, out_part = pl.pallas_call(
        pointwise_kernel,
        name="pointwise",
        grid=(rows,),
        in_specs=[
            row_spec(channels), row_spec(channels), row_spec(channels), row_spec(1),
            whole(channels, 1), whole(channels, 1), whole(channels, wide), whole(wide, channels),
            whole(wide, 1), whole(channels, wide), whole(wide, channels), whole(channels, 1),
        ],
        out_specs=[
            row_spec(channels), row_spec(channels), whole(channels, wide), whole(channels, wide),
            whole(channels, 1), whole(channels, 1), whole(wide, 1), whole(channels, 1),
        ],
        out_shape=[
            jax.ShapeDtypeStruct((rows, channels, lon), bf16),
            jax.ShapeDtypeStruct((rows, channels, lon), bf16),
            jax.ShapeDtypeStruct((channels, wide), f32),
            jax.ShapeDtypeStruct((channels, wide), f32),
            jax.ShapeDtypeStruct((channels, 1), f32),
            jax.ShapeDtypeStruct((channels, 1), f32),
            jax.ShapeDtypeStruct((wide, 1), f32),
            jax.ShapeDtypeStruct((channels, 1), f32),
        ],
        compiler_params=params,
    )(
        conv_out, own, cot_rows, ocean_mask[:, None, :], column(norm_gain), column(norm_shift),
        widen, widen.T, column(hidden_offset), narrow, narrow.T, column(output_offset),
    )

    g_above, g_below = halos(conv_back, devices)
    grad_rows, pairs = pl.pallas_call(
        back_kernel,
        name="depthwise_back",
        grid=(groups,),
        in_specs=[
            rows_spec(RIM), rows_spec(rows), rows_spec(RIM),
            rows_spec(RIM), rows_spec(rows), rows_spec(RIM),
            rows_spec(rows), band_spec,
        ],
        out_specs=[rows_spec(rows), pl.BlockSpec((1, rows, span), lambda g: (g, 0, 0))],
        out_shape=[
            jax.ShapeDtypeStruct((rows, channels, lon), bf16),
            jax.ShapeDtypeStruct((groups, rows, span), f32),
        ],
        scratch_shapes=[pltpu.VMEM((span, lon), bf16)],
        compiler_params=params,
    )(above, own, below, g_above, conv_back, g_below, cot_rows, band_back)

    fields_grad = lax.all_to_all(
        jnp.swapaxes(grad_rows, 0, 1)[None], "sp", split_axis=1, concat_axis=2, tiled=True
    )

    pairs = pairs.reshape(groups, rows, KS, rows + KS - 1, GROUP)
    taps = sum(pairs[:, h, :, h : h + KS, :] for h in range(rows))
    kernel_part = jnp.transpose(taps, (0, 3, 2, 1)).reshape(channels, KS * KS)
    tail = -(2 * wide + KS * KS) % 128
    joined = jnp.concatenate(
        [widen_part, narrow_part, kernel_part, jnp.zeros((channels, tail), f32)], axis=1
    )
    summed = lax.psum_scatter(joined, "sp", scatter_dimension=0, tiled=True) * grad_scale
    small = jnp.concatenate([gain_part[:, 0], shift_part[:, 0], hidden_part[:, 0], out_part[:, 0]])
    small = jnp.sum(lax.all_gather(small, "sp"), axis=0) * grad_scale
    edges = np.cumsum([channels, channels, wide])
    gain_sum, shift_sum, hidden_sum, output_sum = jnp.split(small, edges)
    return (
        jnp.swapaxes(updated, 0, 1)[None],
        fields_grad,
        summed[:, 2 * wide : 2 * wide + KS * KS].reshape(-1, KS, KS),
        summed[:, :wide],
        summed[:, wide : 2 * wide],
        gain_sum,
        shift_sum,
        hidden_sum,
        output_sum,
    )


def solution(mesh):
    return jax.shard_map(
        local,
        mesh=mesh,
        in_specs=(
            P("groups", "sp", None, None),
            P("groups", None, "sp", None),
            P("sp", None),
            P("groups", None, None),
            P("groups"),
            P("groups"),
            P("groups", None),
            P("groups"),
            P("groups", None),
            P("groups"),
        ),
        out_specs=(
            P("groups", None, "sp", None),
            P("groups", "sp", None, None),
            P(("groups", "sp"), None, None),
            P(("groups", "sp"), None),
            P(("groups", "sp"), None),
            P("groups"),
            P("groups"),
            P("groups"),
            P("groups"),
        ),
        check_vma=False,
    )
```

time: 442 us -> 338 us (0.76)
  the two profiles are of different devices: /device:TPU:0 before, /device:TPU:13 now
where the time goes in v1:
time: 338 us; the launch traced here: 335 us
  waiting for transfers between devices  98.2 us (29%)
  blocking collectives  84.7 us (25%)
  local copies, waits for them, and re-layouts  49.3 us (15%)
  Pallas kernels  48.7 us (14%)
  starting transfers between devices  34.4 us (10%)
  between operations  15.4 us (5%)
    unnamed x2, waiting for transfers between devices  87.4 us
    all_to_all x1, blocking collectives, local(): own = lax.all_to_all(fields, 'sp', split_axis=2, concat_axis=1, tiled=True)  42.4 us
    all_gather x1, blocking collectives, local(): small = jnp.sum(lax.all_gather(small, 'sp'), axis=0) * grad_scale  42.3 us
    pallas_call x1, Pallas kernels, local(): pl.pallas_call(back_kernel, name='depthwise_back', grid=(groups,), in_spe...  21.3 us
    all_to_all x1, starting transfers between devices, local(): lax.all_to_all(jnp.swapaxes(grad_rows, 0, 1)[None], 'sp', split_axis=1, c...  15.9 us
    pallas_call x1, Pallas kernels, local(): pl.pallas_call(pointwise_kernel, name='pointwise', grid=(rows,), in_specs...  15 us
    unnamed x92, local copies, waits for them, and re-layouts  13.2 us
    ppermute x2, starting transfers between devices, halos(): lax.ppermute(values[:RIM], 'sp', [(d + 1, d) for d in range(devices - 1)])  13 us
  transfers between devices with their start and end apart: 6, of which 4 were waited for; matrix products, arithmetic and copies ran while one was open for 8% of the time, Pallas kernels for 0%

profile of v1, /device:TPU:13, one launch (start us, length us, event | category | flops | bytes accessed | tf_op | source)
XLA Modules:
  0.0 335.0 jit_solution(13767688404996384605)
XLA Ops:
  7.2 2.3 copy.66
  9.5 42.4 %all_to_all.33 = bf16[1,8,64,1440]{3,1,0,2:T(8,128)(2,1)S(1)} all-to-all(bf16[1,8,64,1440]{3,1,0,2:T(8,128)(2,1)S(1)} %copy.66), channel_id=1, replica_groups=mesh['groups'=2,'sp'=16] {'sp'}, dimensions={2} | all-to-all | bytes 2949120 | tf_op jit(solution)/shard_map/all_to_all | solution.py:141
  52.2 0.9 copy-done.30
  53.1 1.4 copy.69
  54.6 1.4 copy.68
  56.0 3.6 %collective-permute-start = (bf16[3,128,1440]{1,2,0:T(8,128)(2,1)}, bf16[3,128,1440]{1,2,0:T(8,128)(2,1)}, u32[]{:S(2)}, u32[]{:S(2)}) collective-permute-start(bf16[3,128,1440]{1,2,0:T(8,128)(2,1)} %copy.68), channel_id=1, source_target_pairs={{0,1},{1,2},{2,3},{3,4},{4,5},{5,6},{6,7},{7,8},{8,9},{9,10},{10,1... | collective-permute-start | bytes 3317768 | tf_op jit(solution)/shard_map/ppermute | solution.py:120
  59.6 1.9 collective-permute-start.1
  62.2 0.7 copy.80.gain
  63.0 0.7 copy.81.shift
  63.7 0.7 copy.83.out_off
  64.4 0.7 copy.78
  65.2 0.7 copy.79
  65.9 0.8 copy.82.hidden_off
  66.7 0.7 fusion.25
  67.5 1.6 copy.77
  69.9 2.4 collective-permute-done
  72.3 1.6 copy.75.above.x_above
  73.9 3.8 %collective-permute-done.1 = bf16[3,128,1440]{1,2,0:T(8,128)(2,1)} collective-permute-done((bf16[3,128,1440]{1,2,0:T(8,128)(2,1)}, bf16[3,128,1440]{1,2,0:T(8,128)(2,1)}, u32[]{:S(2)}, u32[]{:S(2)}) %collective-permute-start.1) | collective-permute-done | bytes 1105952 | tf_op jit(solution)/shard_map/ppermute | solution.py:121
  77.7 1.6 copy.76.below.x_below
  79.3 12.5 %depthwise.1.conv = bf16[4,128,1440]{2,1,0:T(8,128)(2,1)S(1)} custom-call(bf16[3,128,1440]{2,1,0:T(8,128)(2,1)S(1)} %copy.75.above.x_above, bf16[4,128,1440]{2,1,0:T(8,128)(2,1)} %bitcast.65, bf16[3,128,1440]{2,1,0:T(8,128)(2,1)S(1)} %copy.76.below.x_below, bf16[4,128,1120]{2,1,0:T(8,128)(2,1)S(1)} %fusion.band), custom_call_target="tpu_custom_call" | custom-call | tf_op jit(solution)/shard_map/depthwise/pallas_call | solution.py:149
  91.9 15.0 %pointwise.1 = (bf16[4,128,1440]{2,1,0:T(8,128)(2,1)S(1)}, bf16[4,128,1440]{2,1,0:T(8,128)(2,1)S(1)}, f32[128,256]{1,0:T(8,128)S(1)}, f32[128,256]{1,0:T(8,128)S...) custom-call(bf16[4,128,1440]{2,1,0:T(8,128)(2,1)S(1)} %depthwise.1.conv, ...), custom_call_target="tpu_custom_call" | custom-call | tf_op jit(solution)/shard_map/pointwise/pallas_call | solution.py:167
  107.0 1.4 fusion.22
  109.1 2.4 copy.84
  111.5 1.9 collective-permute-start.2
  113.4 1.4 copy.85
  114.8 11.1 %collective-permute-start.3 = (bf16[3,128,1440]{1,2,0:T(8,128)(2,1)}, bf16[3,128,1440]{1,2,0:T(8,128)(2,1)}, u32[]{:S(2)}, u32[]{:S(2)}) collective-permute-start(bf16[3,128,1440]{1,2,0:T(8,128)(2,1)} %copy.85), channel_id=1, source_target_pairs={{1,0},{2,1},{3,2},{4,3},{5,4},{6,5},{7,6},{8,7},{9,8},{10,9},{11,1... | collective-permute-start | bytes 3317768 | tf_op jit(solution)/shard_map/ppermute | solution.py:121
  125.9 1.4 stack.35
  127.3 1.4 stack.38
  128.6 1.4 stack.37
  130.0 1.4 stack.36
  131.4 1.6 fusion.1.band
  133.0 2.4 copy.93.g_above
  135.3 4.5 %collective-permute-done.3 = bf16[3,128,1440]{1,2,0:T(8,128)(2,1)} collective-permute-done((bf16[3,128,1440]{1,2,0:T(8,128)(2,1)}, bf16[3,128,1440]{1,2,0:T(8,128)(2,1)}, u32[]{:S(2)}, u32[]{:S(2)}) %collective-permute-start.3) | collective-permute-done | bytes 1105952 | tf_op jit(solution)/shard_map/ppermute | solution.py:121
  139.9 2.4 copy.94.g_below
  142.3 1.3 copy-done.1
  143.6 1.3 copy-done.2
  144.8 21.3 %depthwise_back.1 = (bf16[4,128,1440]{2,1,0:T(8,128)(2,1)}, f32[8,4,1120]{2,1,0:T(4,128)S(1)}) custom-call(bf16[3,128,1440]{2,1,0:T(8,128)(2,1)S(1)} %copy.75.above.x_above, bf16[4,128,1440]{2,1,0:T(8,128)(2,1)} %bitcast.67, bf16[3,128,1440]{2,1,0:T(8,128)(2,1)S(1)} %copy.76.below.x_below, bf16[3,128,1440]{2,1,0:T(8,128)(2,1)S(1)} %copy-done.1, ...), custom_call_target="tpu_custom_call" | custom-call | tf_op jit(solution)/shard_map/depthwise_back/pallas_call | solution.py:197
  166.1 0.6 copy-done.15
  166.8 3.8 %copy.95 = bf16[1,128,4,1440]{3,2,0,1:T(4,128)(2,1)} copy(bf16[1,128,4,1440]{3,1,2,0:T(8,128)(2,1)} %bitcast.71) | data formatting | bytes 2949120 | tf_op jit(solution)/shard_map/broadcast_in_dim | solution.py:216
  170.5 15.9 %all-to-all-start.1 = ((bf16[1,128,4,1440]{3,2,0,1:T(4,128)(2,1)}), bf16[1,128,4,1440]{3,2,0,1:T(4,128)(2,1)}, u32[]{:S(2)}, u32[]{:S(2)}) async-start(bf16[1,128,4,1440]{3,2,0,1:T(4,128)(2,1)} %copy.95), calls=%async_computation.1 | async-start | bytes 3145728 | tf_op jit(solution)/shard_map/all_to_all | solution.py:215
  187.8 1.6 copy.100
  189.8 42.3 %all-gather.1 = f32[16,1,640]{2,1,0:T(1,128)S(1)} all-gather(f32[1,1,640]{2,1,0:T(1,128)S(1)} %reshape.118), channel_id=2, replica_groups=mesh['groups'=2,'sp'=16] {'sp'}, dimensions={0}, use_global_device_ids=true | all-gather | bytes 43520 | tf_op jit(solution)/shard_map/all_gather | solution.py:228
  233.7 0.7 maximum_maximum_fusion
  235.0 87.4 %all-reduce.11.cloned.1.call-done = f32[128,640]{1,0:T(8,128)} async-done(((f32[128,640]{1,0:T(8,128)}), f32[128,640]{1,0:T(8,128)}) %all-reduce.11.cloned.1.call-update) | async-done | bytes 327696
  322.5 0.7 dynamic-slice_multiply_fusion
  323.3 0.6 copy.101
  324.5 1.9 copy.96
  326.5 1.6 all_to_all.30
  (119 shorter events, 6.6 us)
Async XLA Ops:
  52.0 1.1 copy-start.30
  54.5 7.0 %copy-start.34 = (f32[128,7,7]{0,2,1:T(8,128)S(1)}, f32[128,7,7]{0,2,1:T(8,128)}, u32[]{:S(2)}) copy-start(f32[128,7,7]{0,2,1:T(8,128)} %param.15) | copy-start | bytes 75268
  54.5 7.1 %copy-start.35 = (s32[4,1440]{1,0:T(4,128)S(1)}, s32[4,1440]{1,0:T(4,128)}, u32[]{:S(2)}) copy-start(s32[4,1440]{1,0:T(4,128)} %param.14) | copy-start | bytes 69124
  54.5 7.7 %copy-start.37 = (f32[128]{0:T(128)S(1)}, f32[128]{0:T(128)}, u32[]{:S(2)}) copy-start(f32[128]{0:T(128)} %param.16) | copy-start | bytes 1540
  54.5 8.4 %copy-start.38 = (f32[128]{0:T(128)S(1)}, f32[128]{0:T(128)}, u32[]{:S(2)}) copy-start(f32[128]{0:T(128)} %param.17) | copy-start | bytes 1540
  54.5 9.2 %copy-start.39 = (f32[128]{0:T(128)S(1)}, f32[128]{0:T(128)}, u32[]{:S(2)}) copy-start(f32[128]{0:T(128)} %param.21) | copy-start | bytes 1540
  54.5 9.9 %copy-start.6 = (bf16[128,256]{1,0:T(8,128)(2,1)S(1)}, bf16[128,256]{1,0:T(8,128)(2,1)}, u32[]{:S(2)}) copy-start(bf16[128,256]{1,0:T(8,128)(2,1)} %widen.1) | copy-start | bytes 196612
  54.6 10.6 %copy-start.8 = (bf16[128,256]{1,0:T(8,128)(2,1)S(1)}, bf16[128,256]{1,0:T(8,128)(2,1)}, u32[]{:S(2)}) copy-start(bf16[128,256]{1,0:T(8,128)(2,1)} %narrow.1) | copy-start | bytes 196612
  54.6 11.3 %copy-start.36 = (f32[256]{0:T(256)S(1)}, f32[256]{0:T(256)}, u32[]{:S(2)}) copy-start(f32[256]{0:T(256)} %param.19) | copy-start | bytes 3076
  54.6 12.9 %copy-start.31 = (bf16[1,128,4,1440]{1,3,2,0:T(8,128)(2,1)S(1)}, bf16[1,128,4,1440]{1,3,2,0:T(8,128)(2,1)}, u32[]{:S(2)}) copy-start(bf16[1,128,4,1440]{1,3,2,0:T(8,128)(2,1)} %param.13) | copy-start | bytes 4423684
  56.0 16.3 %collective-permute-start = (bf16[3,128,1440]{1,2,0:T(8,128)(2,1)}, bf16[3,128,1440]{1,2,0:T(8,128)(2,1)}, u32[]{:S(2)}, u32[]{:S(2)}) collective-permute-start(bf16[3,128,1440]{1,2,0:T(8,128)(2,1)} %copy.68), channel_id=1, source_target_pairs={{0,1},{1,2},{2,3},{3,4},{4,5},{5,6},{6,7},{7,8},{8,9},{9,10},{10,1... | collective-permute-start | bytes 3317768 | tf_op jit(solution)/shard_map/ppermute | solution.py:120
  59.6 18.1 %collective-permute-start.1 = (bf16[3,128,1440]{1,2,0:T(8,128)(2,1)}, bf16[3,128,1440]{1,2,0:T(8,128)(2,1)}, u32[]{:S(2)}, u32[]{:S(2)}) collective-permute-start(bf16[3,128,1440]{1,2,0:T(8,128)(2,1)} %copy.69), channel_id=1, source_target_pairs={{1,0},{2,1},{3,2},{4,3},{5,4},{6,5},{7,6},{8,7},{9,8},{10,9},{11,1... | collective-permute-start | bytes 3317768 | tf_op jit(solution)/shard_map/ppermute | solution.py:121
  67.4 1.8 copy-start.33
  69.2 0.7 copy-start.32
  79.2 12.6 %copy-start.5 = (f32[256,1]{1,0:T(8,128)S(1)}, f32[256,1]{1,0:T(8,128)}, u32[]{:S(2)}) copy-start(f32[256,1]{1,0:T(8,128)} %copy.82.hidden_off) | copy-start | bytes 3076
  79.2 12.6 %copy-start.7 = (bf16[128,256]{1,0:T(8,128)(2,1)S(1)}, bf16[128,256]{1,0:T(8,128)(2,1)}, u32[]{:S(2)}) copy-start(bf16[128,256]{1,0:T(8,128)(2,1)} %widen.1) | copy-start | bytes 196612
  79.3 12.6 %copy-start.9 = (bf16[128,256]{1,0:T(8,128)(2,1)S(1)}, bf16[128,256]{1,0:T(8,128)(2,1)}, u32[]{:S(2)}) copy-start(bf16[128,256]{1,0:T(8,128)(2,1)} %narrow.1) | copy-start | bytes 196612
  79.3 12.6 %copy-start.10 = (f32[128,1]{1,0:T(8,128)S(1)}, f32[128,1]{1,0:T(8,128)}, u32[]{:S(2)}) copy-start(f32[128,1]{1,0:T(8,128)} %copy.80.gain) | copy-start | bytes 1540
  79.3 12.6 %copy-start.11 = (f32[128,1]{1,0:T(8,128)S(1)}, f32[128,1]{1,0:T(8,128)}, u32[]{:S(2)}) copy-start(f32[128,1]{1,0:T(8,128)} %copy.81.shift) | copy-start | bytes 1540
  79.3 12.6 %copy-start.12 = (f32[128,1]{1,0:T(8,128)S(1)}, f32[128,1]{1,0:T(8,128)}, u32[]{:S(2)}) copy-start(f32[128,1]{1,0:T(8,128)} %copy.83.out_off) | copy-start | bytes 1540
  79.3 12.6 %copy-start.13 = (bf16[128,256]{0,1:T(8,128)(2,1)S(1)}, bf16[128,256]{0,1:T(8,128)(2,1)}, u32[]{:S(2)}) copy-start(bf16[128,256]{0,1:T(8,128)(2,1)} %copy.78) | copy-start | bytes 196612
  79.3 12.6 %copy-start.14 = (bf16[128,256]{0,1:T(8,128)(2,1)S(1)}, bf16[128,256]{0,1:T(8,128)(2,1)}, u32[]{:S(2)}) copy-start(bf16[128,256]{0,1:T(8,128)(2,1)} %copy.79) | copy-start | bytes 196612
  79.3 12.6 %copy-start.23 = (s32[4,1,1440]{2,1,0:T(1,128)S(1)}, s32[4,1,1440]{2,1,0:T(1,128)}, u32[]{:S(2)}) copy-start(s32[4,1,1440]{2,1,0:T(1,128)} %broadcast_in_dim.50.mask) | copy-start | bytes 69124
  106.9 1.5 copy-start
  106.9 2.0 copy-start.3
  106.9 2.0 copy-start.17
  106.9 2.1 copy-start.19
  106.9 2.1 copy-start.21
  106.9 2.1 copy-start.24
  106.9 2.1 copy-start.26
  106.9 2.1 copy-start.28
  111.5 21.5 %collective-permute-start.2 = (bf16[3,128,1440]{1,2,0:T(8,128)(2,1)}, bf16[3,128,1440]{1,2,0:T(8,128)(2,1)}, u32[]{:S(2)}, u32[]{:S(2)}) collective-permute-start(bf16[3,128,1440]{1,2,0:T(8,128)(2,1)} %copy.84), channel_id=1, source_target_pairs={{0,1},{1,2},{2,3},{3,4},{4,5},{5,6},{6,7},{7,8},{8,9},{9,10},{10,1... | collective-permute-start | bytes 3317768 | tf_op jit(solution)/shard_map/ppermute | solution.py:120
  114.8 25.0 %collective-permute-start.3 = (bf16[3,128,1440]{1,2,0:T(8,128)(2,1)}, bf16[3,128,1440]{1,2,0:T(8,128)(2,1)}, u32[]{:S(2)}, u32[]{:S(2)}) collective-permute-start(bf16[3,128,1440]{1,2,0:T(8,128)(2,1)} %copy.85), channel_id=1, source_target_pairs={{1,0},{2,1},{3,2},{4,3},{5,4},{6,5},{7,6},{8,7},{9,8},{10,9},{11,1... | collective-permute-start | bytes 3317768 | tf_op jit(solution)/shard_map/ppermute | solution.py:121
  142.3 1.3 copy-start.1
  143.6 1.3 copy-start.2
  166.1 0.6 copy-start.15
  170.5 15.9 %copy-start.40 = (u32[32]{0:T(128)S(1)}, u32[32]{0:T(128)}, u32[]{:S(2)}) copy-start(u32[32]{0:T(128)} %constant.65) | copy-start | bytes 388
  170.5 17.2 %copy-start.4 = (bf16[4,128,1440]{2,1,0:T(8,128)(2,1)S(1)}, bf16[4,128,1440]{2,1,0:T(8,128)(2,1)}, u32[]{:S(2)}) copy-start(bf16[4,128,1440]{2,1,0:T(8,128)(2,1)} %copy-done.3) | copy-start | bytes 4423684
  170.5 154.0 %all-to-all-start.1 = ((bf16[1,128,4,1440]{3,2,0,1:T(4,128)(2,1)}), bf16[1,128,4,1440]{3,2,0,1:T(4,128)(2,1)}, u32[]{:S(2)}, u32[]{:S(2)}) async-start(bf16[1,128,4,1440]{3,2,0,1:T(4,128)(2,1)} %copy.95), calls=%async_computation.1 | async-start | bytes 3145728 | tf_op jit(solution)/shard_map/all_to_all | solution.py:215
  186.4 136.1 %all-reduce.11.cloned.1.call-start = ((), (), s32[]{:S(2)}) async-start(), calls=%async_computation.2 | async-start | bytes 655360
  187.8 1.6 copy-start.29
  187.8 1.7 copy-start.27
  187.8 1.8 copy-start.25
  187.8 1.9 copy-start.22
  187.8 45.0 %copy-start.16 = (f32[8,4,1120]{2,1,0:T(4,128)S(1)}, f32[8,4,1120]{2,1,0:T(4,128)}, u32[]{:S(2)}) copy-start(f32[8,4,1120]{2,1,0:T(4,128)} %copy-done.15) | copy-start | bytes 430084
  232.8 1.0 copy-start.18
  232.8 1.0 copy-start.20
Sparse Core Ops, SparseCore 0:
  234.6 87.7 all-reduce.10

commit v2 on v1

--- a/solution.py
+++ b/solution.py
@@ -51,16 +51,19 @@
     out[...] = result.astype(out.dtype).reshape(rows, group, lon)
 
 
-def back_kernel(x_above, x_own, x_below, g_above, g_own, g_below, cotangent, band, out, parts, scratch):
-    rows, group, lon = x_own.shape
-    grads = g_own[...].reshape(rows * group, lon)
-    shifts(jnp.concatenate([x_above[...], x_own[...], x_below[...]], axis=0), scratch)
-    pairs = dot_nt(grads, scratch[...])
+def tap_kernel(above, own, below, grads, parts, scratch):
+    rows, group, lon = own.shape
+    shifts(jnp.concatenate([above[...], own[...], below[...]], axis=0), scratch)
+    pairs = dot_nt(grads[...].reshape(rows * group, lon), scratch[...])
     row = lax.broadcasted_iota(jnp.int32, pairs.shape, 0) % group
     col = lax.broadcasted_iota(jnp.int32, pairs.shape, 1) % group
     kept = jnp.where(row == col, pairs, 0.0)
     parts[...] = jnp.sum(kept.reshape(rows, group, -1), axis=1)[None]
-    shifts(jnp.concatenate([g_above[...], g_own[...], g_below[...]], axis=0), scratch)
+
+
+def back_kernel(above, own, below, cotangent, band, out, scratch):
+    rows, group, lon = own.shape
+    shifts(jnp.concatenate([above[...], own[...], below[...]], axis=0), scratch)
     spread = dot(band[...].reshape(rows * group, -1), scratch[...])
     total = cotangent[...].reshape(rows * group, lon).astype(jnp.float32) + spread
     out[...] = total.astype(out.dtype).reshape(rows, group, lon)
@@ -132,6 +135,9 @@
     grad_scale = 1.0 / math.sqrt(samples * rows * devices * lon)
     groups = channels // GROUP
     span = KS * (rows + KS - 1) * GROUP
+    cost = pl.CostEstimate(
+        flops=2 * rows * GROUP * span * lon * groups, bytes_accessed=4 * rows * channels * lon * 3, transcendentals=0
+    )
     params = pltpu.CompilerParams(vmem_limit_bytes=48 * 1024 * 1024)
 
     band = band_matrix(kernel, rows)
@@ -194,46 +200,58 @@
     )
 
     g_above, g_below = halos(conv_back, devices)
-    grad_rows, pairs = pl.pallas_call(
+    pairs = pl.pallas_call(
+        tap_kernel,
+        name="tap_grads",
+        grid=(groups,),
+        in_specs=[rows_spec(RIM), rows_spec(rows), rows_spec(RIM), rows_spec(rows)],
+        out_specs=pl.BlockSpec((1, rows, span), lambda g: (g, 0, 0)),
+        out_shape=jax.ShapeDtypeStruct((groups, rows, span), f32),
+        scratch_shapes=[pltpu.VMEM((span, lon), bf16)],
+        compiler_params=params,
+        cost_estimate=cost,
+    )(above, own, below, conv_back)
+
+    pairs = pairs.reshape(groups, rows, KS, rows + KS - 1, GROUP)
+    taps = sum(pairs[:, h, :, h : h + KS, :] for h in range(rows))
+    kernel_part = jnp.transpose(taps, (0, 3, 2, 1)).reshape(channels, KS * KS)
+    small = jnp.concatenate([gain_part[:, 0], shift_part[:, 0], hidden_part[:, 0], out_part[:, 0]])
+    pieces = [
+        part.reshape(devices, -1)
+        for part in (widen_part, narrow_part, jnp.pad(kernel_part, ((0, 0), (0, 128 - KS * KS))))
+    ]
+    pieces.append(jnp.broadcast_to(small[None], (devices, small.shape[0])))
+    joined = jnp.concatenate([piece.reshape(devices, -1, 128) for piece in pieces], axis=1)
+    joined = lax.all_to_all(joined, "sp", split_axis=0, concat_axis=0, tiled=True)
+    summed = jnp.sum(joined, axis=0) * grad_scale
+
+    grad_rows = pl.pallas_call(
         back_kernel,
         name="depthwise_back",
         grid=(groups,),
-        in_specs=[
-            rows_spec(RIM), rows_spec(rows), rows_spec(RIM),
-            rows_spec(RIM), rows_spec(rows), rows_spec(RIM),
-            rows_spec(rows), band_spec,
-        ],
-        out_specs=[rows_spec(rows), pl.BlockSpec((1, rows, span), lambda g: (g, 0, 0))],
-        out_shape=[
-            jax.ShapeDtypeStruct((rows, channels, lon), bf16),
-            jax.ShapeDtypeStruct((groups, rows, span), f32),
-        ],
+        in_specs=[rows_spec(RIM), rows_spec(rows), rows_spec(RIM), rows_spec(rows), band_spec],
+        out_specs=rows_spec(rows),
+        out_shape=jax.ShapeDtypeStruct((rows, channels, lon), bf16),
         scratch_shapes=[pltpu.VMEM((span, lon), bf16)],
         compiler_params=params,
-    )(above, own, below, g_above, conv_back, g_below, cot_rows, band_back)
+        cost_estimate=cost,
+    )(g_above, conv_back, g_below, cot_rows, band_back)
 
     fields_grad = lax.all_to_all(
         jnp.swapaxes(grad_rows, 0, 1)[None], "sp", split_axis=1, concat_axis=2, tiled=True
     )
 
-    pairs = pairs.reshape(groups, rows, KS, rows + KS - 1, GROUP)
-    taps = sum(pairs[:, h, :, h : h + KS, :] for h in range(rows))
-    kernel_part = jnp.transpose(taps, (0, 3, 2, 1)).reshape(channels, KS * KS)
-    tail = -(2 * wide + KS * KS) % 128
-    joined = jnp.concatenate(
-        [widen_part, narrow_part, kernel_part, jnp.zeros((channels, tail), f32)], axis=1
-    )
-    summed = lax.psum_scatter(joined, "sp", scatter_dimension=0, tiled=True) * grad_scale
-    small = jnp.concatenate([gain_part[:, 0], shift_part[:, 0], hidden_part[:, 0], out_part[:, 0]])
-    small = jnp.sum(lax.all_gather(small, "sp"), axis=0) * grad_scale
-    edges = np.cumsum([channels, channels, wide])
-    gain_sum, shift_sum, hidden_sum, output_sum = jnp.split(small, edges)
+    own_channels = channels // devices
+    edges = np.cumsum([own_channels * wide // 128, own_channels * wide // 128, own_channels])
+    widen_sum, narrow_sum, kernel_sum, small_sum = jnp.split(summed, edges)
+    small_sum = small_sum.reshape(-1)
+    gain_sum, shift_sum, hidden_sum, output_sum = jnp.split(small_sum, np.cumsum([channels, channels, wide]))
     return (
         jnp.swapaxes(updated, 0, 1)[None],
         fields_grad,
-        summed[:, 2 * wide : 2 * wide + KS * KS].reshape(-1, KS, KS),
-        summed[:, :wide],
-        summed[:, wide : 2 * wide],
+        kernel_sum[:, : KS * KS].reshape(-1, KS, KS),
+        widen_sum.reshape(-1, wide),
+        narrow_sum.reshape(-1, wide),
         gain_sum,
         shift_sum,
         hidden_sum,

time: 338 us -> 225 us (0.67)
  waiting for transfers between devices: 98.2 us -> 51.6 us
  blocking collectives: 84.7 us -> 42.4 us
  local copies, waits for them, and re-layouts: 49.3 us -> 32.3 us
  between operations: 15.4 us -> 1.34 us
  other arithmetic: 2.19 us -> 7.05 us
  Pallas kernels: 48.7 us -> 52.5 us
    unnamed x2 -> x0, waiting for transfers between devices: 87.4 us -> none
    all_gather x1 -> x0, blocking collectives: 42.3 us -> none  [local(): small = jnp.sum(lax.all_gather(small, 'sp'), axis=0) * grad_scale]
    all_to_all x1, waiting for transfers between devices: 0.01 us -> 30.6 us  [local(): lax.all_to_all(jnp.swapaxes(grad_rows, 0, 1)[None], 'sp', split_axis=1, c...]
    pallas_call x0 -> x1, Pallas kernels: none -> 12.4 us  [local(): pl.pallas_call(tap_kernel, name='tap_grads', grid=(groups,), in_specs=[ro...]
    pallas_call x1, Pallas kernels: 21.3 us -> 12.5 us  [local(): pl.pallas_call(back_kernel, name='depthwise_back', grid=(groups,), in_spe...]
    ppermute x2, waiting for transfers between devices: 8.31 us -> 16.6 us  [halos(): lax.ppermute(values[:RIM], 'sp', [(d + 1, d) for d in range(devices - 1)])]
    all_to_all x0 -> x1, starting transfers between devices: none -> 5.59 us  [local(): lax.all_to_all(joined, 'sp', split_axis=0, concat_axis=0, tiled=True)]
    another operation x8, local copies, waits for them, and re-layouts: 5.51 us -> 0.11 us  [band_matrix(): jnp.stack([jnp.pad(taps, ((0, 0), (0, 0), (h, rows - 1 - h))) for h in ra...]
  transfers between devices with their start and end apart: 6 -> 6, of which waited for: 4 -> 4; matrix products, arithmetic and copies ran while one was open for 8% -> 10% of each run, Pallas kernels for 0% -> 6%
where the time goes in v2:
time: 225 us
  Pallas kernels  52.5 us (23%)
  waiting for transfers between devices  51.6 us (23%)
  blocking collectives  42.4 us (19%)
  starting transfers between devices  35.3 us (16%)
  local copies, waits for them, and re-layouts  32.3 us (14%)
  other arithmetic  7.05 us (3%)
    all_to_all x1, blocking collectives, local(): own = lax.all_to_all(fields, 'sp', split_axis=2, concat_axis=1, tiled=True)  42.4 us
    all_to_all x1, waiting for transfers between devices, local(): lax.all_to_all(jnp.swapaxes(grad_rows, 0, 1)[None], 'sp', split_axis=1, c...  30.6 us
    ppermute x2, waiting for transfers between devices, halos(): lax.ppermute(values[:RIM], 'sp', [(d + 1, d) for d in range(devices - 1)])  16.6 us
    pallas_call x1, Pallas kernels, local(): pl.pallas_call(pointwise_kernel, name='pointwise', grid=(rows,), in_specs...  15.1 us
    pallas_call x1, Pallas kernels, local(): pl.pallas_call(conv_kernel, name='depthwise', grid=(groups,), in_specs=[r...  12.5 us
    pallas_call x1, Pallas kernels, local(): pl.pallas_call(back_kernel, name='depthwise_back', grid=(groups,), in_spe...  12.5 us
    pallas_call x1, Pallas kernels, local(): pl.pallas_call(tap_kernel, name='tap_grads', grid=(groups,), in_specs=[ro...  12.4 us
    all_to_all x1, starting transfers between devices, local(): lax.all_to_all(jnp.swapaxes(grad_rows, 0, 1)[None], 'sp', split_axis=1, c...  12.3 us
  transfers between devices with their start and end apart: 6, of which 4 were waited for; matrix products, arithmetic and copies ran while one was open for 10% of the time, Pallas kernels for 6%

profile of v2, /device:TPU:13, one launch (start us, length us, event | category | flops | bytes accessed | tf_op | source)
XLA Modules:
  0.0 224.5 jit_solution(16501916423341570548)
XLA Ops:
  0.6 2.3 %copy.88 = bf16[1,8,64,1440]{3,1,0,2:T(8,128)(2,1)S(1)} copy(bf16[1,8,64,1440]{3,2,1,0:T(8,128)(2,1)} %param.12) | data formatting | bytes 2949120 | tf_op args[0]
  2.9 42.4 %all_to_all.38 = bf16[1,8,64,1440]{3,1,0,2:T(8,128)(2,1)S(1)} all-to-all(bf16[1,8,64,1440]{3,1,0,2:T(8,128)(2,1)S(1)} %copy.88), channel_id=1, replica_groups=mesh['groups'=2,'sp'=16] {'sp'}, dimensions={2} | all-to-all | bytes 2949120 | tf_op jit(solution)/shard_map/all_to_all | solution.py:147
  45.5 0.2 fusion.23
  45.7 0.9 copy-done
  46.6 1.4 copy.90
  48.0 3.8 %collective-permute-start = (bf16[3,128,1440]{1,2,0:T(8,128)(2,1)}, bf16[3,128,1440]{1,2,0:T(8,128)(2,1)}, u32[]{:S(2)}, u32[]{:S(2)}) collective-permute-start(bf16[3,128,1440]{1,2,0:T(8,128)(2,1)} %copy.90), channel_id=1, source_target_pairs={{0,1},{1,2},{2,3},{3,4},{4,5},{5,6},{6,7},{7,8},{8,9},{9,10},{10,1... | collective-permute-start | bytes 3317768 | tf_op jit(solution)/shard_map/ppermute | solution.py:123
  51.8 1.4 copy.91
  53.2 1.9 collective-permute-start.1
  55.2 0.6 fusion.25
  56.0 1.6 copy.99
  58.5 1.5 fusion.band
  60.1 4.4 %collective-permute-done = bf16[3,128,1440]{1,2,0:T(8,128)(2,1)} collective-permute-done((bf16[3,128,1440]{1,2,0:T(8,128)(2,1)}, bf16[3,128,1440]{1,2,0:T(8,128)(2,1)}, u32[]{:S(2)}, u32[]{:S(2)}) %collective-permute-start) | collective-permute-done | bytes 1105952 | tf_op jit(solution)/shard_map/ppermute | solution.py:123
  64.5 1.6 copy.97.above
  66.0 5.2 %collective-permute-done.1 = bf16[3,128,1440]{1,2,0:T(8,128)(2,1)} collective-permute-done((bf16[3,128,1440]{1,2,0:T(8,128)(2,1)}, bf16[3,128,1440]{1,2,0:T(8,128)(2,1)}, u32[]{:S(2)}, u32[]{:S(2)}) %collective-permute-start.1) | collective-permute-done | bytes 1105952 | tf_op jit(solution)/shard_map/ppermute | solution.py:124
  71.2 1.6 copy.98.below
  72.8 1.3 copy-done.5
  74.1 12.5 %depthwise.1.conv = bf16[4,128,1440]{2,1,0:T(8,128)(2,1)S(1)} custom-call(bf16[3,128,1440]{2,1,0:T(8,128)(2,1)S(1)} %copy.97.above, bf16[4,128,1440]{2,1,0:T(8,128)(2,1)} %bitcast.73, bf16[3,128,1440]{2,1,0:T(8,128)(2,1)S(1)} %copy.98.below, bf16[4,128,1120]{2,1,0:T(8,128)(2,1)S(1)} %copy-done.5), custom_call_target="tpu_custom_call" | custom-call | tf_op jit(solution)/shard_map/depthwise/pallas_call | solution.py:155
  86.6 15.1 %pointwise.1 = (bf16[4,128,1440]{2,1,0:T(8,128)(2,1)S(1)}, bf16[4,128,1440]{2,1,0:T(8,128)(2,1)S(1)}, f32[128,256]{1,0:T(8,128)S(1)}, f32[128,256]{1,0:T(8,128)S...) custom-call(bf16[4,128,1440]{2,1,0:T(8,128)(2,1)S(1)} %depthwise.1.conv, ...), custom_call_target="tpu_custom_call" | custom-call | tf_op jit(solution)/shard_map/pointwise/pallas_call | solution.py:173
  101.9 12.4 %tap_grads.1 = f32[8,4,1120]{2,1,0:T(4,128)S(1)} custom-call(bf16[3,128,1440]{2,1,0:T(8,128)(2,1)S(1)} %copy.97.above, bf16[4,128,1440]{2,1,0:T(8,128)(2,1)S(1)} %bitcast.75, bf16[3,128,1440]{2,1,0:T(8,128)(2,1)S(1)} %copy-done.4, bf16[4,128,1440]{2,1,0:T(8,128)(2,1)S(1)} %get-tuple-element.18.own.grads), custom_call_target="tpu_custom_call" | custom-call | flops 1651507200 | bytes 8847360 | tf_op jit(solution)/shard_map/tap_grads/pallas_call | solution.py:203
  114.3 1.2 fusion.22
  115.5 1.1 reduce.2
  116.6 1.0 reduce
  117.6 1.5 reduce.1
  119.1 1.5 reduce.3
  120.5 1.8 reshape.132
  122.4 1.4 copy.106
  123.7 2.0 collective-permute-start.2
  125.8 1.4 copy.107
  127.2 9.7 %collective-permute-start.3 = (bf16[3,128,1440]{1,2,0:T(8,128)(2,1)}, bf16[3,128,1440]{1,2,0:T(8,128)(2,1)}, u32[]{:S(2)}, u32[]{:S(2)}) collective-permute-start(bf16[3,128,1440]{1,2,0:T(8,128)(2,1)} %copy.107), channel_id=1, source_target_pairs={{1,0},{2,1},{3,2},{4,3},{5,4},{6,5},{7,6},{8,7},{9,8},{10,9},{11,1... | collective-permute-start | bytes 3317768 | tf_op jit(solution)/shard_map/ppermute | solution.py:124
  137.3 0.8 pad_maximum_fusion
  138.1 5.6 %all-to-all-start.2 = ((f32[16,45,128]{2,1,0:T(8,128)}), f32[16,45,128]{2,1,0:T(8,128)}, u32[]{:S(2)}, u32[]{:S(2)}) async-start(f32[16,45,128]{2,1,0:T(8,128)} %pad_maximum_fusion), calls=%async_computation.2 | async-start | bytes 786432 | tf_op jit(solution)/shard_map/all_to_all | solution.py:225
  143.8 0.5 fusion.1.band
  144.3 1.6 copy.113.above
  145.9 11.4 %collective-permute-done.3 = bf16[3,128,1440]{1,2,0:T(8,128)(2,1)} collective-permute-done((bf16[3,128,1440]{1,2,0:T(8,128)(2,1)}, bf16[3,128,1440]{1,2,0:T(8,128)(2,1)}, u32[]{:S(2)}, u32[]{:S(2)}) %collective-permute-start.3) | collective-permute-done | bytes 1105952 | tf_op jit(solution)/shard_map/ppermute | solution.py:124
  157.3 1.6 copy.114.below
  158.9 12.5 %depthwise_back.1 = bf16[4,128,1440]{2,1,0:T(8,128)(2,1)S(1)} custom-call(bf16[3,128,1440]{2,1,0:T(8,128)(2,1)S(1)} %copy.113.above, bf16[4,128,1440]{2,1,0:T(8,128)(2,1)} %copy-done.2, bf16[3,128,1440]{2,1,0:T(8,128)(2,1)S(1)} %copy.114.below, bf16[4,128,1440]{2,1,0:T(8,128)(2,1)} %bitcast.81, bf16[4,128,1120]{2,1,0:T(8,128)(2,1)S(1)} %fusion.1.band), custom_call_target="tpu_custom_call" | custom-call | flops 1651507200 | bytes 8847360 | tf_op jit(solution)/shard_map/depthwise_back/pallas_call | solution.py:228
  171.4 2.4 %copy.115 = bf16[1,128,4,1440]{3,2,0,1:T(4,128)(2,1)} copy(bf16[1,128,4,1440]{3,1,2,0:T(8,128)(2,1)S(1)} %bitcast.76) | data formatting | bytes 2949120 | tf_op jit(solution)/shard_map/broadcast_in_dim | solution.py:241
  173.8 12.3 %all-to-all-start.1 = ((bf16[1,128,4,1440]{3,2,0,1:T(4,128)(2,1)}), bf16[1,128,4,1440]{3,2,0,1:T(4,128)(2,1)S(1)}, u32[]{:S(2)}, u32[]{:S(2)}) async-start(bf16[1,128,4,1440]{3,2,0,1:T(4,128)(2,1)} %copy.115), calls=%async_computation.1 | async-start | bytes 3145728 | tf_op jit(solution)/shard_map/all_to_all | solution.py:240
  186.1 1.6 copy.122
  187.7 1.0 reduce_sum.9
  188.8 0.6 copy.123
  189.4 0.6 reshape.135
  190.0 0.6 reshape.136
  190.6 0.6 slice_bitcast_fusion
  191.2 0.5 slice_bitcast_fusion.1
  191.7 30.6 %all-to-all-done.1 = bf16[1,128,4,1440]{3,2,0,1:T(4,128)(2,1)S(1)} async-done(((bf16[1,128,4,1440]{3,2,0,1:T(4,128)(2,1)}), bf16[1,128,4,1440]{3,2,0,1:T(4,128)(2,1)S(1)}, u32[]{:S(2)}, u32[]{:S(2)}) %all-to-all-start.1) | async-done | bytes 1474592 | tf_op jit(solution)/shard_map/all_to_all | solution.py:240
  222.3 0.5 copy.116
  222.9 1.6 all_to_all.33
  (95 shorter events, 1.8 us)
Async XLA Ops:
  45.5 1.1 copy-start
  48.0 7.1 %copy-start.20 = (f32[128,7,7]{0,2,1:T(8,128)S(1)}, f32[128,7,7]{0,2,1:T(8,128)}, u32[]{:S(2)}) copy-start(f32[128,7,7]{0,2,1:T(8,128)} %param.15) | copy-start | bytes 75268
  48.0 7.9 %copy-start.18 = (bf16[1,128,4,1440]{1,3,2,0:T(8,128)(2,1)S(1)}, bf16[1,128,4,1440]{1,3,2,0:T(8,128)(2,1)}, u32[]{:S(2)}) copy-start(bf16[1,128,4,1440]{1,3,2,0:T(8,128)(2,1)} %param.13) | copy-start | bytes 4423684
  48.0 16.5 %collective-permute-start = (bf16[3,128,1440]{1,2,0:T(8,128)(2,1)}, bf16[3,128,1440]{1,2,0:T(8,128)(2,1)}, u32[]{:S(2)}, u32[]{:S(2)}) collective-permute-start(bf16[3,128,1440]{1,2,0:T(8,128)(2,1)} %copy.90), channel_id=1, source_target_pairs={{0,1},{1,2},{2,3},{3,4},{4,5},{5,6},{6,7},{7,8},{8,9},{9,10},{10,1... | collective-permute-start | bytes 3317768 | tf_op jit(solution)/shard_map/ppermute | solution.py:123
  53.2 18.0 %collective-permute-start.1 = (bf16[3,128,1440]{1,2,0:T(8,128)(2,1)}, bf16[3,128,1440]{1,2,0:T(8,128)(2,1)}, u32[]{:S(2)}, u32[]{:S(2)}) collective-permute-start(bf16[3,128,1440]{1,2,0:T(8,128)(2,1)} %copy.91), channel_id=1, source_target_pairs={{1,0},{2,1},{3,2},{4,3},{5,4},{6,5},{7,6},{8,7},{9,8},{10,9},{11,1... | collective-permute-start | bytes 3317768 | tf_op jit(solution)/shard_map/ppermute | solution.py:124
  55.9 1.7 copy-start.25
  55.9 1.8 copy-start.8
  55.9 1.9 copy-start.9
  55.9 2.0 copy-start.26
  55.9 2.2 copy-start.27
  56.0 2.3 %copy-start.28 = (f32[128]{0:T(128)S(1)}, f32[128]{0:T(128)}, u32[]{:S(2)}) copy-start(f32[128]{0:T(128)} %param.21) | copy-start | bytes 1540
  56.0 2.4 %copy-start.22 = (s32[4,1440]{1,0:T(4,128)S(1)}, s32[4,1440]{1,0:T(4,128)}, u32[]{:S(2)}) copy-start(s32[4,1440]{1,0:T(4,128)} %param.14) | copy-start | bytes 69124
  56.0 2.6 %copy-start.19 = (bf16[70,1120,1]{1,0,2:T(8,128)(2,1)S(1)}, bf16[70,1120,1]{1,0,2:T(8,128)(2,1)}, u32[]{:S(2)}) copy-start(bf16[70,1120,1]{1,0,2:T(8,128)(2,1)} %constant.63) | copy-start | bytes 470404
  72.8 1.3 copy-start.5
  74.1 12.6 %copy-start.3 = (bf16[3,128,1440]{2,1,0:T(8,128)(2,1)}, bf16[3,128,1440]{2,1,0:T(8,128)(2,1)S(1)}, u32[]{:S(2)}) copy-start(bf16[3,128,1440]{2,1,0:T(8,128)(2,1)S(1)} %copy.98.below) | copy-start | bytes 3317764
  86.6 15.2 %copy-start.1 = (bf16[1,8,16,4,1440]{4,1,2,3,0:T(8,128)(2,1)S(1)}, bf16[1,8,16,4,1440]{4,1,2,3,0:T(8,128)(2,1)}, u32[]{:S(2)}) copy-start(bf16[1,8,16,4,1440]{4,1,2,3,0:T(8,128)(2,1)} %copy-done) | copy-start | bytes 4423684
  86.6 15.2 %copy-start.4 = (bf16[3,128,1440]{2,1,0:T(8,128)(2,1)S(1)}, bf16[3,128,1440]{2,1,0:T(8,128)(2,1)}, u32[]{:S(2)}) copy-start(bf16[3,128,1440]{2,1,0:T(8,128)(2,1)} %copy-done.3) | copy-start | bytes 3317764
  101.8 12.5 %copy-start.2 = (bf16[4,128,1440]{2,1,0:T(8,128)(2,1)}, bf16[4,128,1440]{2,1,0:T(8,128)(2,1)S(1)}, u32[]{:S(2)}) copy-start(bf16[4,128,1440]{2,1,0:T(8,128)(2,1)S(1)} %get-tuple-element.18.own.grads) | copy-start | bytes 4423684
  101.8 12.5 %copy-start.6 = (bf16[4,128,1440]{2,1,0:T(8,128)(2,1)}, bf16[4,128,1440]{2,1,0:T(8,128)(2,1)S(1)}, u32[]{:S(2)}) copy-start(bf16[4,128,1440]{2,1,0:T(8,128)(2,1)S(1)} %get-tuple-element.17) | copy-start | bytes 4423684
  101.8 12.5 %copy-start.10 = (f32[128,256]{1,0:T(8,128)}, f32[128,256]{1,0:T(8,128)S(1)}, u32[]{:S(2)}) copy-start(f32[128,256]{1,0:T(8,128)S(1)} %get-tuple-element.20) | copy-start | bytes 393220
  101.8 12.5 %copy-start.12 = (f32[256,1]{1,0:T(8,128)}, f32[256,1]{1,0:T(8,128)S(1)}, u32[]{:S(2)}) copy-start(f32[256,1]{1,0:T(8,128)S(1)} %get-tuple-element.23) | copy-start | bytes 3076
  101.8 12.5 %copy-start.13 = (f32[128,1]{1,0:T(8,128)}, f32[128,1]{1,0:T(8,128)S(1)}, u32[]{:S(2)}) copy-start(f32[128,1]{1,0:T(8,128)S(1)} %get-tuple-element.24) | copy-start | bytes 1540
  101.8 12.5 %copy-start.14 = (f32[128,1]{1,0:T(8,128)}, f32[128,1]{1,0:T(8,128)S(1)}, u32[]{:S(2)}) copy-start(f32[128,1]{1,0:T(8,128)S(1)} %get-tuple-element.22) | copy-start | bytes 1540
  101.8 12.5 %copy-start.15 = (f32[128,1]{1,0:T(8,128)}, f32[128,1]{1,0:T(8,128)S(1)}, u32[]{:S(2)}) copy-start(f32[128,1]{1,0:T(8,128)S(1)} %get-tuple-element.21) | copy-start | bytes 1540
  115.5 6.9 %copy-start.16 = (bf16[3,128,1440]{2,1,0:T(8,128)(2,1)S(1)}, bf16[3,128,1440]{2,1,0:T(8,128)(2,1)}, u32[]{:S(2)}) copy-start(bf16[3,128,1440]{2,1,0:T(8,128)(2,1)} %get-tuple-element.62) | copy-start | bytes 3317764
  123.7 13.1 %copy-start.17 = (f32[8,4,7,10,16]{4,3,2,0,1:T(8,128)S(1)}, f32[8,4,7,10,16]{4,3,2,0,1:T(8,128)}, u32[]{:S(2)}) copy-start(f32[8,4,7,10,16]{4,3,2,0,1:T(8,128)} %reshape.132) | copy-start | bytes 430084
  123.7 20.6 %collective-permute-start.2 = (bf16[3,128,1440]{1,2,0:T(8,128)(2,1)}, bf16[3,128,1440]{1,2,0:T(8,128)(2,1)}, u32[]{:S(2)}, u32[]{:S(2)}) collective-permute-start(bf16[3,128,1440]{1,2,0:T(8,128)(2,1)} %copy.106), channel_id=1, source_target_pairs={{0,1},{1,2},{2,3},{3,4},{4,5},{5,6},{6,7},{7,8},{8,9},{9,10},{10,1... | collective-permute-start | bytes 3317768 | tf_op jit(solution)/shard_map/ppermute | solution.py:123
  127.2 10.0 %copy-start.11 = (f32[128,256]{1,0:T(8,128)S(1)}, f32[128,256]{1,0:T(8,128)}, u32[]{:S(2)}) copy-start(f32[128,256]{1,0:T(8,128)} %copy-done.10) | copy-start | bytes 393220
  127.2 10.1 %copy-start.23 = (f32[128]{0:T(128)S(1)}, f32[128]{0:T(128)}, u32[]{:S(2)}) copy-start(f32[128]{0:T(128)} %reduce.1) | copy-start | bytes 1540
  127.2 10.1 %copy-start.24 = (f32[128]{0:T(128)S(1)}, f32[128]{0:T(128)}, u32[]{:S(2)}) copy-start(f32[128]{0:T(128)} %reduce.3) | copy-start | bytes 1540
  127.2 30.1 %collective-permute-start.3 = (bf16[3,128,1440]{1,2,0:T(8,128)(2,1)}, bf16[3,128,1440]{1,2,0:T(8,128)(2,1)}, u32[]{:S(2)}, u32[]{:S(2)}) collective-permute-start(bf16[3,128,1440]{1,2,0:T(8,128)(2,1)} %copy.107), channel_id=1, source_target_pairs={{1,0},{2,1},{3,2},{4,3},{5,4},{6,5},{7,6},{8,7},{9,8},{10,9},{11,1... | collective-permute-start | bytes 3317768 | tf_op jit(solution)/shard_map/ppermute | solution.py:124
  136.9 6.8 %copy-start.21 = (bf16[128,7,10]{0,2,1:T(8,128)(2,1)S(1)}, bf16[128,7,10]{0,2,1:T(8,128)(2,1)}, u32[]{:S(2)}) copy-start(bf16[128,7,10]{0,2,1:T(8,128)(2,1)} %get-tuple-element.70) | copy-start | bytes 53764
  138.1 35.7 %all-to-all-start.2 = ((f32[16,45,128]{2,1,0:T(8,128)}), f32[16,45,128]{2,1,0:T(8,128)}, u32[]{:S(2)}, u32[]{:S(2)}) async-start(f32[16,45,128]{2,1,0:T(8,128)} %pad_maximum_fusion), calls=%async_computation.2 | async-start | bytes 786432 | tf_op jit(solution)/shard_map/all_to_all | solution.py:225
  173.8 12.3 %copy-start.7 = (bf16[4,128,1440]{2,1,0:T(8,128)(2,1)S(1)}, bf16[4,128,1440]{2,1,0:T(8,128)(2,1)}, u32[]{:S(2)}) copy-start(bf16[4,128,1440]{2,1,0:T(8,128)(2,1)} %copy-done.6) | copy-start | bytes 4423684
  173.8 48.5 %all-to-all-start.1 = ((bf16[1,128,4,1440]{3,2,0,1:T(4,128)(2,1)}), bf16[1,128,4,1440]{3,2,0,1:T(4,128)(2,1)S(1)}, u32[]{:S(2)}, u32[]{:S(2)}) async-start(bf16[1,128,4,1440]{3,2,0,1:T(4,128)(2,1)} %copy.115), calls=%async_computation.1 | async-start | bytes 3145728 | tf_op jit(solution)/shard_map/all_to_all | solution.py:240

commit v3 on v2

--- a/solution.py
+++ b/solution.py
@@ -6,6 +6,7 @@
 import numpy as np
 from jax import lax
 from jax.experimental import pallas as pl
+from jax.experimental.layout import Layout, with_layout_constraint
 from jax.experimental.pallas import tpu as pltpu
 from jax.sharding import PartitionSpec as P
 
@@ -58,7 +59,11 @@
     row = lax.broadcasted_iota(jnp.int32, pairs.shape, 0) % group
     col = lax.broadcasted_iota(jnp.int32, pairs.shape, 1) % group
     kept = jnp.where(row == col, pairs, 0.0)
-    parts[...] = jnp.sum(kept.reshape(rows, group, -1), axis=1)[None]
+    total = jnp.sum(kept[:group], axis=0, keepdims=True)
+    for h in range(1, rows):
+        line = jnp.sum(kept[h * group : (h + 1) * group], axis=0, keepdims=True)
+        total += jnp.concatenate([line[:, h * group :], line[:, : h * group]], axis=1)
+    parts[...] = total[None]
 
 
 def back_kernel(above, own, below, cotangent, band, out, scratch):
@@ -120,8 +125,13 @@
 
 
 def halos(values, devices):
-    above = lax.ppermute(values[-RIM:], "sp", [(d, d + 1) for d in range(devices - 1)])
-    below = lax.ppermute(values[:RIM], "sp", [(d + 1, d) for d in range(devices - 1)])
+    def send(piece, pairs):
+        piece = with_layout_constraint(piece, Layout(major_to_minor=(0, 1, 2)))
+        piece = lax.ppermute(piece, "sp", pairs)
+        return with_layout_constraint(piece, Layout(major_to_minor=(0, 1, 2)))
+
+    above = send(values[-RIM:], [(d, d + 1) for d in range(devices - 1)])
+    below = send(values[:RIM], [(d + 1, d) for d in range(devices - 1)])
     return above, below
 
 
@@ -136,7 +146,7 @@
     groups = channels // GROUP
     span = KS * (rows + KS - 1) * GROUP
     cost = pl.CostEstimate(
-        flops=2 * rows * GROUP * span * lon * groups, bytes_accessed=4 * rows * channels * lon * 3, transcendentals=0
+        flops=20 * rows * GROUP * span * lon * groups, bytes_accessed=4 * rows * channels * lon * 3, transcendentals=0
     )
     params = pltpu.CompilerParams(vmem_limit_bytes=48 * 1024 * 1024)
 
@@ -205,15 +215,14 @@
         name="tap_grads",
         grid=(groups,),
         in_specs=[rows_spec(RIM), rows_spec(rows), rows_spec(RIM), rows_spec(rows)],
-        out_specs=pl.BlockSpec((1, rows, span), lambda g: (g, 0, 0)),
-        out_shape=jax.ShapeDtypeStruct((groups, rows, span), f32),
+        out_specs=pl.BlockSpec((1, 1, span), lambda g: (g, 0, 0)),
+        out_shape=jax.ShapeDtypeStruct((groups, 1, span), f32),
         scratch_shapes=[pltpu.VMEM((span, lon), bf16)],
         compiler_params=params,
         cost_estimate=cost,
     )(above, own, below, conv_back)
 
-    pairs = pairs.reshape(groups, rows, KS, rows + KS - 1, GROUP)
-    taps = sum(pairs[:, h, :, h : h + KS, :] for h in range(rows))
+    taps = pairs.reshape(groups, KS, rows + KS - 1, GROUP)[:, :, :KS]
     kernel_part = jnp.transpose(taps, (0, 3, 2, 1)).reshape(channels, KS * KS)
     small = jnp.concatenate([gain_part[:, 0], shift_part[:, 0], hidden_part[:, 0], out_part[:, 0]])
     pieces = [

time: 225 us -> 208 us (0.924)
  blocking collectives: 42.4 us -> 0 us
  waiting for transfers between devices: 51.6 us -> 74.2 us
  local copies, waits for them, and re-layouts: 32.3 us -> 37.7 us
  other arithmetic: 7.05 us -> 2.51 us
    all_to_all x1 -> x0, blocking collectives: 42.4 us -> none  [local(): own = lax.all_to_all(fields, 'sp', split_axis=2, concat_axis=1, tiled=True)]
    all_to_all x0 -> x1, waiting for transfers between devices: none -> 36.1 us  [local(): own = lax.all_to_all(fields, 'sp', split_axis=2, concat_axis=1, tiled=True)]
    ppermute x4, waiting for transfers between devices: 21 us -> 7.56 us  [send(): piece = lax.ppermute(piece, 'sp', pairs)]
    another operation x0 -> x4, local copies, waits for them, and re-layouts: none -> 7.1 us  [send(): piece = with_layout_constraint(piece, Layout(major_to_minor=(0, 1, 2)))]
    all_to_all x0 -> x1, starting transfers between devices: none -> 6.69 us  [local(): own = lax.all_to_all(fields, 'sp', split_axis=2, concat_axis=1, tiled=True)]
    all_to_all x1, starting transfers between devices: 12.3 us -> 6.15 us  [local(): lax.all_to_all(jnp.swapaxes(grad_rows, 0, 1)[None], 'sp', split_axis=1, c...]
    unnamed x67 -> x51, local copies, waits for them, and re-layouts: 8.69 us -> 13.4 us
    pallas_call x4, other arithmetic: 4.99 us -> 0.43 us  [local(): pl.pallas_call(pointwise_kernel, name='pointwise', grid=(rows,), in_specs...]
  transfers between devices with their start and end apart: 6 -> 7, of which waited for: 4 -> 4; matrix products, arithmetic and copies ran while one was open for 10% -> 12% of each run, Pallas kernels for 6% -> 12%
where the time goes in v3:
time: 208 us; the launch traced here: 207 us
  waiting for transfers between devices  74.2 us (36%)
  Pallas kernels  52.8 us (25%)
  local copies, waits for them, and re-layouts  37.7 us (18%)
  starting transfers between devices  35.3 us (17%)
  matrix products  3.08 us (1%)
  other arithmetic  2.51 us (1%)
    all_to_all x1, waiting for transfers between devices, local(): own = lax.all_to_all(fields, 'sp', split_axis=2, concat_axis=1, tiled=True)  36.1 us
    all_to_all x1, waiting for transfers between devices, local(): lax.all_to_all(jnp.swapaxes(grad_rows, 0, 1)[None], 'sp', split_axis=1, c...  30.6 us
    ppermute x4, starting transfers between devices, send(): piece = lax.ppermute(piece, 'sp', pairs)  16.9 us
    pallas_call x1, Pallas kernels, local(): pl.pallas_call(pointwise_kernel, name='pointwise', grid=(rows,), in_specs...  14.9 us
    unnamed x51, local copies, waits for them, and re-layouts  13.4 us
    pallas_call x1, Pallas kernels, local(): pl.pallas_call(tap_kernel, name='tap_grads', grid=(groups,), in_specs=[ro...  12.8 us
    pallas_call x1, Pallas kernels, local(): pl.pallas_call(conv_kernel, name='depthwise', grid=(groups,), in_specs=[r...  12.6 us
    pallas_call x1, Pallas kernels, local(): pl.pallas_call(back_kernel, name='depthwise_back', grid=(groups,), in_spe...  12.5 us
  transfers between devices with their start and end apart: 7, of which 4 were waited for; matrix products, arithmetic and copies ran while one was open for 12% of the time, Pallas kernels for 12%

profile of v3, /device:TPU:13, one launch (start us, length us, event | category | flops | bytes accessed | tf_op | source)
XLA Modules:
  0.0 206.9 jit_solution(18055321239611131191)
XLA Ops:
  0.6 3.4 %copy.86 = bf16[1,8,64,1440]{3,1,0,2:T(8,128)(2,1)} copy(bf16[1,8,64,1440]{3,2,1,0:T(8,128)(2,1)} %param.12) | data formatting | bytes 2949120 | tf_op args[0]
  4.1 6.7 %all-to-all-start = ((bf16[1,8,64,1440]{3,1,0,2:T(8,128)(2,1)}), bf16[1,8,64,1440]{3,1,0,2:T(8,128)(2,1)S(1)}, u32[]{:S(2)}, u32[]{:S(2)}) async-start(bf16[1,8,64,1440]{3,1,0,2:T(8,128)(2,1)} %copy.86), calls=%async_computation | async-start | bytes 3145728 | tf_op jit(solution)/shard_map/all_to_all | solution.py:157
  10.9 36.1 %all-to-all-done = bf16[1,8,64,1440]{3,1,0,2:T(8,128)(2,1)S(1)} async-done(((bf16[1,8,64,1440]{3,1,0,2:T(8,128)(2,1)}), bf16[1,8,64,1440]{3,1,0,2:T(8,128)(2,1)S(1)}, u32[]{:S(2)}, u32[]{:S(2)}) %all-to-all-start) | async-done | bytes 1474592 | tf_op jit(solution)/shard_map/all_to_all | solution.py:157
  46.9 0.1 copy.131
  47.1 1.4 fusion.22
  48.6 1.9 copy.88
  50.5 3.6 %collective-permute-start = (bf16[3,128,1440]{1,2,0:T(8,128)(2,1)S(1)}, bf16[3,128,1440]{1,2,0:T(8,128)(2,1)}, u32[]{:S(2)}, u32[]{:S(2)}) collective-permute-start(bf16[3,128,1440]{1,2,0:T(8,128)(2,1)S(1)} %copy.88), channel_id=1, source_target_pairs={{0,1},{1,2},{2,3},{3,4},{4,5},{5,6},{6,7},{7,8},{8,9},{9,10},{10,1... | collective-permute-start | bytes 3317768 | tf_op jit(solution)/shard_map/ppermute | solution.py:130
  54.1 1.4 copy.90
  55.5 1.9 collective-permute-start.1
  57.6 2.7 %copy.97 = bf16[1,128,4,1440]{3,1,2,0:T(8,128)(2,1)} copy(bf16[1,128,4,1440]{1,3,2,0:T(8,128)(2,1)} %param.13) | data formatting | bytes 2949120 | tf_op args[1]
  60.3 0.1 copy.102.hidden_off
  61.2 0.1 broadcast_compare_fusion
  61.3 1.5 fusion.band
  62.8 1.6 fusion.1.band
  64.4 2.1 %collective-permute-done = bf16[3,128,1440]{1,2,0:T(8,128)(2,1)} collective-permute-done((bf16[3,128,1440]{1,2,0:T(8,128)(2,1)S(1)}, bf16[3,128,1440]{1,2,0:T(8,128)(2,1)}, u32[]{:S(2)}, u32[]{:S(2)}) %collective-permute-start) | collective-permute-done | bytes 1105952 | tf_op jit(solution)/shard_map/ppermute | solution.py:130
  66.5 1.6 copy.89.above
  68.1 5.5 %collective-permute-done.1 = bf16[3,128,1440]{1,2,0:T(8,128)(2,1)} collective-permute-done((bf16[3,128,1440]{1,2,0:T(8,128)(2,1)}, bf16[3,128,1440]{1,2,0:T(8,128)(2,1)}, u32[]{:S(2)}, u32[]{:S(2)}) %collective-permute-start.1) | collective-permute-done | bytes 1105952 | tf_op jit(solution)/shard_map/ppermute | solution.py:130
  73.5 1.6 copy.91.below
  75.1 1.3 copy-done.4
  76.4 12.6 %depthwise.1.conv = bf16[4,128,1440]{2,1,0:T(8,128)(2,1)S(1)} custom-call(bf16[3,128,1440]{2,1,0:T(8,128)(2,1)S(1)} %copy.89.above, bf16[4,128,1440]{2,1,0:T(8,128)(2,1)} %bitcast.69, bf16[3,128,1440]{2,1,0:T(8,128)(2,1)S(1)} %copy.91.below, bf16[4,128,1120]{2,1,0:T(8,128)(2,1)S(1)} %copy-done.4), custom_call_target="tpu_custom_call" | custom-call | tf_op jit(solution)/shard_map/depthwise/pallas_call | solution.py:165
  88.9 14.9 %pointwise.1 = (bf16[4,128,1440]{2,1,0:T(8,128)(2,1)S(1)}, bf16[4,128,1440]{2,1,0:T(8,128)(2,1)S(1)}, f32[128,256]{1,0:T(8,128)S(1)}, f32[128,256]{1,0:T(8,128)S...) custom-call(bf16[4,128,1440]{2,1,0:T(8,128)(2,1)S(1)} %depthwise.1.conv, ...), custom_call_target="tpu_custom_call" | custom-call | tf_op jit(solution)/shard_map/pointwise/pallas_call | solution.py:183
  103.9 1.4 fusion.21
  105.4 0.5 copy-done.7
  105.9 1.4 copy.104
  107.4 2.0 collective-permute-start.2
  109.4 2.4 %copy.106 = bf16[3,128,1440]{1,2,0:T(8,128)(2,1)} copy(bf16[3,128,1440]{2,1,0:T(8,128)(2,1)} %get-tuple-element.61) | data formatting | bytes 2211840 | tf_op jit(solution)/shard_map/layout_constraint | solution.py:129
  111.8 9.4 %collective-permute-start.3 = (bf16[3,128,1440]{1,2,0:T(8,128)(2,1)}, bf16[3,128,1440]{1,2,0:T(8,128)(2,1)}, u32[]{:S(2)}, u32[]{:S(2)}) collective-permute-start(bf16[3,128,1440]{1,2,0:T(8,128)(2,1)} %copy.106), channel_id=1, source_target_pairs={{1,0},{2,1},{3,2},{4,3},{5,4},{6,5},{7,6},{8,7},{9,8},{10,9},{11,1... | collective-permute-start | bytes 3317768 | tf_op jit(solution)/shard_map/ppermute | solution.py:130
  121.2 1.3 copy-done.3
  122.5 1.4 copy-done.6
  123.9 12.8 %tap_grads.1 = f32[8,1,1120]{2,1,0:T(1,128)S(1)} custom-call(bf16[3,128,1440]{2,1,0:T(8,128)(2,1)S(1)} %copy.89.above, bf16[4,128,1440]{2,1,0:T(8,128)(2,1)S(1)} %bitcast.71, bf16[3,128,1440]{2,1,0:T(8,128)(2,1)S(1)} %copy-done.3, bf16[4,128,1440]{2,1,0:T(8,128)(2,1)S(1)} %copy-done.6), custom_call_target="tpu_custom_call" | custom-call | flops 16515072000 | bytes 8847360 | tf_op jit(solution)/shard_map/tap_grads/pallas_call | solution.py:213
  137.2 0.1 reshape.129
  137.8 0.8 pad_maximum_fusion
  138.6 5.6 %all-to-all-start.2 = ((f32[16,45,128]{2,1,0:T(8,128)}), f32[16,45,128]{2,1,0:T(8,128)}, u32[]{:S(2)}, u32[]{:S(2)}) async-start(f32[16,45,128]{2,1,0:T(8,128)} %pad_maximum_fusion), calls=%async_computation.2 | async-start | bytes 786432 | tf_op jit(solution)/shard_map/all_to_all | solution.py:234
  144.1 1.6 copy.105.above
  145.7 1.7 copy.107.below
  147.4 12.5 %depthwise_back.1 = bf16[4,128,1440]{2,1,0:T(8,128)(2,1)S(1)} custom-call(bf16[3,128,1440]{2,1,0:T(8,128)(2,1)S(1)} %copy.105.above, bf16[4,128,1440]{2,1,0:T(8,128)(2,1)} %copy-done.5, bf16[3,128,1440]{2,1,0:T(8,128)(2,1)S(1)} %copy.107.below, bf16[4,128,1440]{2,1,0:T(8,128)(2,1)} %bitcast.79, bf16[4,128,1120]{2,1,0:T(8,128)(2,1)S(1)} %copy-done.9), custom_call_target="tpu_custom_call" | custom-call | flops 16515072000 | bytes 8847360 | tf_op jit(solution)/shard_map/depthwise_back/pallas_call | solution.py:237
  160.0 2.4 %copy.113 = bf16[1,128,4,1440]{3,2,0,1:T(4,128)(2,1)} copy(bf16[1,128,4,1440]{3,1,2,0:T(8,128)(2,1)S(1)} %bitcast.73) | data formatting | bytes 2949120 | tf_op jit(solution)/shard_map/broadcast_in_dim | solution.py:250
  162.3 6.1 %all-to-all-start.1 = ((bf16[1,128,4,1440]{3,2,0,1:T(4,128)(2,1)}), bf16[1,128,4,1440]{3,2,0,1:T(4,128)(2,1)S(1)}, u32[]{:S(2)}, u32[]{:S(2)}) async-start(bf16[1,128,4,1440]{3,2,0,1:T(4,128)(2,1)} %copy.113), calls=%async_computation.1 | async-start | bytes 3145728 | tf_op jit(solution)/shard_map/all_to_all | solution.py:249
  168.5 1.6 copy.117
  170.0 1.0 reduce_sum.9
  171.2 0.6 copy.118
  171.8 0.6 reshape.132
  172.4 0.6 reshape.133
  173.0 0.6 slice_bitcast_fusion.1
  173.6 0.5 slice_bitcast_fusion.2
  174.1 30.6 %all-to-all-done.1 = bf16[1,128,4,1440]{3,2,0,1:T(4,128)(2,1)S(1)} async-done(((bf16[1,128,4,1440]{3,2,0,1:T(4,128)(2,1)}), bf16[1,128,4,1440]{3,2,0,1:T(4,128)(2,1)S(1)}, u32[]{:S(2)}, u32[]{:S(2)}) %all-to-all-start.1) | async-done | bytes 1474592 | tf_op jit(solution)/shard_map/all_to_all | solution.py:249
  204.7 0.5 copy.114
  205.2 1.6 all_to_all.33
  (80 shorter events, 2.1 us)
Async XLA Ops:
  4.1 6.7 %copy-start.15 = (f32[128,7,7]{0,2,1:T(8,128)S(1)}, f32[128,7,7]{0,2,1:T(8,128)}, u32[]{:S(2)}) copy-start(f32[128,7,7]{0,2,1:T(8,128)} %param.15) | copy-start | bytes 75268
  4.1 42.9 %all-to-all-start = ((bf16[1,8,64,1440]{3,1,0,2:T(8,128)(2,1)}), bf16[1,8,64,1440]{3,1,0,2:T(8,128)(2,1)S(1)}, u32[]{:S(2)}, u32[]{:S(2)}) async-start(bf16[1,8,64,1440]{3,1,0,2:T(8,128)(2,1)} %copy.86), calls=%async_computation | async-start | bytes 3145728 | tf_op jit(solution)/shard_map/all_to_all | solution.py:157
  47.1 1.5 copy-start
  50.5 16.0 %collective-permute-start = (bf16[3,128,1440]{1,2,0:T(8,128)(2,1)S(1)}, bf16[3,128,1440]{1,2,0:T(8,128)(2,1)}, u32[]{:S(2)}, u32[]{:S(2)}) collective-permute-start(bf16[3,128,1440]{1,2,0:T(8,128)(2,1)S(1)} %copy.88), channel_id=1, source_target_pairs={{0,1},{1,2},{2,3},{3,4},{4,5},{5,6},{6,7},{7,8},{8,9},{9,10},{10,1... | collective-permute-start | bytes 3317768 | tf_op jit(solution)/shard_map/ppermute | solution.py:130
  55.5 18.0 %collective-permute-start.1 = (bf16[3,128,1440]{1,2,0:T(8,128)(2,1)}, bf16[3,128,1440]{1,2,0:T(8,128)(2,1)}, u32[]{:S(2)}, u32[]{:S(2)}) collective-permute-start(bf16[3,128,1440]{1,2,0:T(8,128)(2,1)} %copy.90), channel_id=1, source_target_pairs={{1,0},{2,1},{3,2},{4,3},{5,4},{6,5},{7,6},{8,7},{9,8},{10,9},{11,1... | collective-permute-start | bytes 3317768 | tf_op jit(solution)/shard_map/ppermute | solution.py:130
  57.5 2.8 %copy-start.17 = (f32[256]{0:T(256)S(1)}, f32[256]{0:T(256)}, u32[]{:S(2)}) copy-start(f32[256]{0:T(256)} %param.19) | copy-start | bytes 3076
  57.5 2.9 %copy-start.10 = (bf16[128,256]{1,0:T(8,128)(2,1)S(1)}, bf16[128,256]{1,0:T(8,128)(2,1)}, u32[]{:S(2)}) copy-start(bf16[128,256]{1,0:T(8,128)(2,1)} %widen.1) | copy-start | bytes 196612
  57.5 3.0 %copy-start.11 = (bf16[128,256]{1,0:T(8,128)(2,1)S(1)}, bf16[128,256]{1,0:T(8,128)(2,1)}, u32[]{:S(2)}) copy-start(bf16[128,256]{1,0:T(8,128)(2,1)} %narrow.1) | copy-start | bytes 196612
  57.5 3.1 %copy-start.18 = (f32[128]{0:T(128)S(1)}, f32[128]{0:T(128)}, u32[]{:S(2)}) copy-start(f32[128]{0:T(128)} %param.16) | copy-start | bytes 1540
  57.5 3.2 %copy-start.19 = (f32[128]{0:T(128)S(1)}, f32[128]{0:T(128)}, u32[]{:S(2)}) copy-start(f32[128]{0:T(128)} %param.17) | copy-start | bytes 1540
  57.6 3.3 %copy-start.20 = (f32[128]{0:T(128)S(1)}, f32[128]{0:T(128)}, u32[]{:S(2)}) copy-start(f32[128]{0:T(128)} %param.21) | copy-start | bytes 1540
  57.6 3.5 %copy-start.16 = (s32[4,1440]{1,0:T(4,128)S(1)}, s32[4,1440]{1,0:T(4,128)}, u32[]{:S(2)}) copy-start(s32[4,1440]{1,0:T(4,128)} %param.14) | copy-start | bytes 69124
  57.6 3.7 %copy-start.14 = (bf16[70,1120,1]{1,0,2:T(8,128)(2,1)S(1)}, bf16[70,1120,1]{1,0,2:T(8,128)(2,1)}, u32[]{:S(2)}) copy-start(bf16[70,1120,1]{1,0,2:T(8,128)(2,1)} %constant.63) | copy-start | bytes 470404
  75.1 1.3 copy-start.4
  76.4 12.6 %copy-start.2 = (bf16[3,128,1440]{2,1,0:T(8,128)(2,1)}, bf16[3,128,1440]{2,1,0:T(8,128)(2,1)S(1)}, u32[]{:S(2)}) copy-start(bf16[3,128,1440]{2,1,0:T(8,128)(2,1)S(1)} %copy.91.below) | copy-start | bytes 3317764
  103.9 1.5 copy-start.5
  103.9 2.1 copy-start.7
  103.9 2.0 copy-start.12
  107.4 13.8 %copy-start.1 = (bf16[1,8,16,4,1440]{4,1,2,3,0:T(8,128)(2,1)S(1)}, bf16[1,8,16,4,1440]{4,1,2,3,0:T(8,128)(2,1)}, u32[]{:S(2)}) copy-start(bf16[1,8,16,4,1440]{4,1,2,3,0:T(8,128)(2,1)} %copy-done) | copy-start | bytes 4423684
  107.4 36.7 %collective-permute-start.2 = (bf16[3,128,1440]{1,2,0:T(8,128)(2,1)}, bf16[3,128,1440]{1,2,0:T(8,128)(2,1)}, u32[]{:S(2)}, u32[]{:S(2)}) collective-permute-start(bf16[3,128,1440]{1,2,0:T(8,128)(2,1)} %copy.104), channel_id=1, source_target_pairs={{0,1},{1,2},{2,3},{3,4},{4,5},{5,6},{6,7},{7,8},{8,9},{9,10},{10,1... | collective-permute-start | bytes 3317768 | tf_op jit(solution)/shard_map/ppermute | solution.py:130
  111.8 33.9 %collective-permute-start.3 = (bf16[3,128,1440]{1,2,0:T(8,128)(2,1)}, bf16[3,128,1440]{1,2,0:T(8,128)(2,1)}, u32[]{:S(2)}, u32[]{:S(2)}) collective-permute-start(bf16[3,128,1440]{1,2,0:T(8,128)(2,1)} %copy.106), channel_id=1, source_target_pairs={{1,0},{2,1},{3,2},{4,3},{5,4},{6,5},{7,6},{8,7},{9,8},{10,9},{11,1... | collective-permute-start | bytes 3317768 | tf_op jit(solution)/shard_map/ppermute | solution.py:130
  121.2 1.3 copy-start.3
  122.5 1.4 copy-start.6
  123.9 12.9 %copy-start.13 = (f32[128,1]{1,0:T(8,128)S(1)}, f32[128,1]{1,0:T(8,128)}, u32[]{:S(2)}) copy-start(f32[128,1]{1,0:T(8,128)} %copy-done.12) | copy-start | bytes 1540
  138.6 23.8 %all-to-all-start.2 = ((f32[16,45,128]{2,1,0:T(8,128)}), f32[16,45,128]{2,1,0:T(8,128)}, u32[]{:S(2)}, u32[]{:S(2)}) async-start(f32[16,45,128]{2,1,0:T(8,128)} %pad_maximum_fusion), calls=%async_computation.2 | async-start | bytes 786432 | tf_op jit(solution)/shard_map/all_to_all | solution.py:234
  145.7 1.7 copy-start.9
  162.3 6.2 %copy-start.8 = (bf16[4,128,1440]{2,1,0:T(8,128)(2,1)S(1)}, bf16[4,128,1440]{2,1,0:T(8,128)(2,1)}, u32[]{:S(2)}) copy-start(bf16[4,128,1440]{2,1,0:T(8,128)(2,1)} %copy-done.7) | copy-start | bytes 4423684
  162.3 42.3 %all-to-all-start.1 = ((bf16[1,128,4,1440]{3,2,0,1:T(4,128)(2,1)}), bf16[1,128,4,1440]{3,2,0,1:T(4,128)(2,1)S(1)}, u32[]{:S(2)}, u32[]{:S(2)}) async-start(bf16[1,128,4,1440]{3,2,0,1:T(4,128)(2,1)} %copy.113), calls=%async_computation.1 | async-start | bytes 3145728 | tf_op jit(solution)/shard_map/all_to_all | solution.py:249

commit v4 on v3

--- a/solution.py
+++ b/solution.py
@@ -6,7 +6,6 @@
 import numpy as np
 from jax import lax
 from jax.experimental import pallas as pl
-from jax.experimental.layout import Layout, with_layout_constraint
 from jax.experimental.pallas import tpu as pltpu
 from jax.sharding import PartitionSpec as P
 
@@ -47,14 +46,14 @@
 
 def conv_kernel(above, own, below, band, out, scratch):
     rows, group, lon = own.shape
-    shifts(jnp.concatenate([above[...], own[...], below[...]], axis=0), scratch)
+    shifts(jnp.concatenate([above[:, :, :lon], own[...], below[:, :, :lon]], axis=0), scratch)
     result = dot(band[...].reshape(rows * group, -1), scratch[...])
     out[...] = result.astype(out.dtype).reshape(rows, group, lon)
 
 
 def tap_kernel(above, own, below, grads, parts, scratch):
     rows, group, lon = own.shape
-    shifts(jnp.concatenate([above[...], own[...], below[...]], axis=0), scratch)
+    shifts(jnp.concatenate([above[:, :, :lon], own[...], below[:, :, :lon]], axis=0), scratch)
     pairs = dot_nt(grads[...].reshape(rows * group, lon), scratch[...])
     row = lax.broadcasted_iota(jnp.int32, pairs.shape, 0) % group
     col = lax.broadcasted_iota(jnp.int32, pairs.shape, 1) % group
@@ -68,7 +67,7 @@
 
 def back_kernel(above, own, below, cotangent, band, out, scratch):
     rows, group, lon = own.shape
-    shifts(jnp.concatenate([above[...], own[...], below[...]], axis=0), scratch)
+    shifts(jnp.concatenate([above[:, :, :lon], own[...], below[:, :, :lon]], axis=0), scratch)
     spread = dot(band[...].reshape(rows * group, -1), scratch[...])
     total = cotangent[...].reshape(rows * group, lon).astype(jnp.float32) + spread
     out[...] = total.astype(out.dtype).reshape(rows, group, lon)
@@ -126,9 +125,8 @@
 
 def halos(values, devices):
     def send(piece, pairs):
-        piece = with_layout_constraint(piece, Layout(major_to_minor=(0, 1, 2)))
-        piece = lax.ppermute(piece, "sp", pairs)
-        return with_layout_constraint(piece, Layout(major_to_minor=(0, 1, 2)))
+        piece = jnp.pad(piece, ((0, 0), (0, 0), (0, -piece.shape[2] % 128)))
+        return lax.ppermute(piece, "sp", pairs)
 
     above = send(values[-RIM:], [(d, d + 1) for d in range(devices - 1)])
     below = send(values[:RIM], [(d + 1, d) for d in range(devices - 1)])
@@ -161,12 +159,13 @@
     def rows_spec(count):
         return pl.BlockSpec((count, GROUP, lon), lambda g: (0, g, 0))
 
+    halo_spec = pl.BlockSpec((RIM, GROUP, above.shape[2]), lambda g: (0, g, 0))
     band_spec = pl.BlockSpec((rows, GROUP, span), lambda g: (0, g, 0))
     conv_out = pl.pallas_call(
         conv_kernel,
         name="depthwise",
         grid=(groups,),
-        in_specs=[rows_spec(RIM), rows_spec(rows), rows_spec(RIM), band_spec],
+        in_specs=[halo_spec, rows_spec(rows), halo_spec, band_spec],
         out_specs=rows_spec(rows),
         out_shape=jax.ShapeDtypeStruct((rows, channels, lon), bf16),
         scratch_shapes=[pltpu.VMEM((span, lon), bf16)],
@@ -214,7 +213,7 @@
         tap_kernel,
         name="tap_grads",
         grid=(groups,),
-        in_specs=[rows_spec(RIM), rows_spec(rows), rows_spec(RIM), rows_spec(rows)],
+        in_specs=[halo_spec, rows_spec(rows), halo_spec, rows_spec(rows)],
         out_specs=pl.BlockSpec((1, 1, span), lambda g: (g, 0, 0)),
         out_shape=jax.ShapeDtypeStruct((groups, 1, span), f32),
         scratch_shapes=[pltpu.VMEM((span, lon), bf16)],
@@ -238,7 +237,7 @@
         back_kernel,
         name="depthwise_back",
         grid=(groups,),
-        in_specs=[rows_spec(RIM), rows_spec(rows), rows_spec(RIM), rows_spec(rows), band_spec],
+        in_specs=[halo_spec, rows_spec(rows), halo_spec, rows_spec(rows), band_spec],
         out_specs=rows_spec(rows),
         out_shape=jax.ShapeDtypeStruct((rows, channels, lon), bf16),
         scratch_shapes=[pltpu.VMEM((span, lon), bf16)],

time: 208 us -> 199 us (0.957)
  local copies, waits for them, and re-layouts: 37.7 us -> 27.6 us
  starting transfers between devices: 35.3 us -> 41.3 us
  waiting for transfers between devices: 74.2 us -> 71.9 us
    all_to_all x1, waiting for transfers between devices: 36.1 us -> 26 us  [local(): own = lax.all_to_all(fields, 'sp', split_axis=2, concat_axis=1, tiled=True)]
    another operation x4 -> x0, local copies, waits for them, and re-layouts: 7.1 us -> none  [send(): piece = with_layout_constraint(piece, Layout(major_to_minor=(0, 1, 2)))]
    ppermute x4, waiting for transfers between devices: 7.56 us -> 14.3 us  [send(): return lax.ppermute(piece, 'sp', pairs)]
    ppermute x4 -> x0, local copies, waits for them, and re-layouts: 6.39 us -> none  [send(): piece = lax.ppermute(piece, 'sp', pairs)]
    all_to_all x1, starting transfers between devices: 6.15 us -> 10.8 us  [local(): lax.all_to_all(jnp.swapaxes(grad_rows, 0, 1)[None], 'sp', split_axis=1, c...]
    unnamed x51 -> x69, local copies, waits for them, and re-layouts: 13.4 us -> 9.14 us
    broadcast_in_dim x4, local copies, waits for them, and re-layouts: 0.47 us -> 4.3 us  [local(): column = lambda vector: vector[:, None]]
    pad x0 -> x4, local copies, waits for them, and re-layouts: none -> 2.44 us  [send(): piece = jnp.pad(piece, ((0, 0), (0, 0), (0, -piece.shape[2] % 128)))]
  transfers between devices with their start and end apart: 7 -> 7, of which waited for: 4 -> 4; matrix products, arithmetic and copies ran while one was open for 12% -> 11% of each run, Pallas kernels for 12% -> 13%
where the time goes in v4:
time: 199 us; the launch traced here: 198 us
  waiting for transfers between devices  71.9 us (36%)
  Pallas kernels  52.7 us (26%)
  starting transfers between devices  41.3 us (21%)
  local copies, waits for them, and re-layouts  27.6 us (14%)
  matrix products  2.04 us (1%)
    all_to_all x1, waiting for transfers between devices, local(): lax.all_to_all(jnp.swapaxes(grad_rows, 0, 1)[None], 'sp', split_axis=1, c...  31.6 us
    all_to_all x1, waiting for transfers between devices, local(): own = lax.all_to_all(fields, 'sp', split_axis=2, concat_axis=1, tiled=True)  26 us
    ppermute x4, starting transfers between devices, send(): return lax.ppermute(piece, 'sp', pairs)  17.9 us
    pallas_call x1, Pallas kernels, local(): pl.pallas_call(pointwise_kernel, name='pointwise', grid=(rows,), in_specs...  15 us
    ppermute x4, waiting for transfers between devices, send(): return lax.ppermute(piece, 'sp', pairs)  14.3 us
    pallas_call x1, Pallas kernels, local(): pl.pallas_call(tap_kernel, name='tap_grads', grid=(groups,), in_specs=[ha...  12.8 us
    pallas_call x1, Pallas kernels, local(): pl.pallas_call(back_kernel, name='depthwise_back', grid=(groups,), in_spe...  12.6 us
    pallas_call x1, Pallas kernels, local(): pl.pallas_call(conv_kernel, name='depthwise', grid=(groups,), in_specs=[h...  12.3 us
  transfers between devices with their start and end apart: 7, of which 4 were waited for; matrix products, arithmetic and copies ran while one was open for 11% of the time, Pallas kernels for 13%

profile of v4, /device:TPU:13, one launch (start us, length us, event | category | flops | bytes accessed | tf_op | source)
XLA Modules:
  0.0 198.4 jit_solution(3412936621124480059)
XLA Ops:
  0.6 3.4 %copy.86 = bf16[1,8,64,1440]{3,1,0,2:T(8,128)(2,1)} copy(bf16[1,8,64,1440]{3,2,1,0:T(8,128)(2,1)} %param.12) | data formatting | bytes 2949120 | tf_op args[0]
  4.1 6.7 %all-to-all-start = ((bf16[1,8,64,1440]{3,1,0,2:T(8,128)(2,1)}), bf16[1,8,64,1440]{3,1,0,2:T(8,128)(2,1)S(1)}, u32[]{:S(2)}, u32[]{:S(2)}) async-start(bf16[1,8,64,1440]{3,1,0,2:T(8,128)(2,1)} %copy.86), calls=%async_computation | async-start | bytes 3145728 | tf_op jit(solution)/shard_map/all_to_all | solution.py:155
  10.9 0.6 stack.30
  11.5 0.6 stack.31
  12.1 0.6 stack.32
  12.7 0.6 stack.33
  13.3 1.6 copy.93
  15.0 0.1 copy.98.hidden_off
  15.3 1.4 copy.96.gain
  16.7 1.4 copy.97.shift
  18.1 1.4 copy.99.out_off
  19.5 1.4 broadcast_in_dim.55.mask
  21.0 26.0 %all-to-all-done = bf16[1,8,64,1440]{3,1,0,2:T(8,128)(2,1)S(1)} async-done(((bf16[1,8,64,1440]{3,1,0,2:T(8,128)(2,1)}), bf16[1,8,64,1440]{3,1,0,2:T(8,128)(2,1)S(1)}, u32[]{:S(2)}, u32[]{:S(2)}) %all-to-all-start) | async-done | bytes 1474592 | tf_op jit(solution)/shard_map/all_to_all | solution.py:155
  46.9 0.1 copy.123
  47.1 0.2 fusion.22
  47.3 0.9 copy-done
  48.4 3.7 %collective-permute-start = (bf16[3,128,1536]{2,1,0:T(8,128)(2,1)S(1)}, bf16[3,128,1536]{2,1,0:T(8,128)(2,1)S(1)}, u32[]{:S(2)}, u32[]{:S(2)}) collective-permute-start(bf16[3,128,1536]{2,1,0:T(8,128)(2,1)S(1)} %pad.53), channel_id=1, source_target_pairs={{0,1},{1,2},{2,3},{3,4},{4,5},{5,6},{6,7},{7,8},{8,9},{9,10},{10,1... | collective-permute-start | bytes 3538952 | tf_op jit(solution)/shard_map/ppermute | solution.py:129
  52.2 1.9 collective-permute-start.1
  54.1 0.1 broadcast_compare_fusion
  54.4 0.5 fusion.band
  54.9 1.5 fusion.1.band
  56.4 8.8 %collective-permute-done.above = bf16[3,128,1536]{2,1,0:T(8,128)(2,1)S(1)} collective-permute-done((bf16[3,128,1536]{2,1,0:T(8,128)(2,1)S(1)}, bf16[3,128,1536]{2,1,0:T(8,128)(2,1)S(1)}, u32[]{:S(2)}, u32[]{:S(2)}) %collective-permute-start) | collective-permute-done | bytes 1179680 | tf_op jit(solution)/shard_map/ppermute | solution.py:129
  65.3 5.5 %collective-permute-done.1.below = bf16[3,128,1536]{2,1,0:T(8,128)(2,1)S(1)} collective-permute-done((bf16[3,128,1536]{2,1,0:T(8,128)(2,1)S(1)}, bf16[3,128,1536]{2,1,0:T(8,128)(2,1)S(1)}, u32[]{:S(2)}, u32[]{:S(2)}) %collective-permute-start.1) | collective-permute-done | bytes 1179680 | tf_op jit(solution)/shard_map/ppermute | solution.py:129
  70.7 12.3 %depthwise.1.conv = bf16[4,128,1440]{2,1,0:T(8,128)(2,1)S(1)} custom-call(bf16[3,128,1536]{2,1,0:T(8,128)(2,1)S(1)} %collective-permute-done.above, bf16[4,128,1440]{2,1,0:T(8,128)(2,1)} %bitcast.69, bf16[3,128,1536]{2,1,0:T(8,128)(2,1)S(1)} %collective-permute-done.1.below, bf16[4,128,1120]{2,1,0:T(8,128)(2,1)S(1)} %fusion.band), custom_call_target="tpu_custom_call" | custom-call | tf_op jit(solution)/shard_map/depthwise/pallas_call | solution.py:164
  83.1 15.0 %pointwise.1 = (bf16[4,128,1440]{2,1,0:T(8,128)(2,1)S(1)}, bf16[4,128,1440]{2,1,0:T(8,128)(2,1)S(1)}, f32[128,256]{1,0:T(8,128)S(1)}, f32[128,256]{1,0:T(8,128)S...) custom-call(bf16[4,128,1440]{2,1,0:T(8,128)(2,1)S(1)} %depthwise.1.conv, ...), custom_call_target="tpu_custom_call" | custom-call | tf_op jit(solution)/shard_map/pointwise/pallas_call | solution.py:182
  98.1 0.2 fusion.21
  98.3 0.4 copy-done.9
  98.9 1.1 pad.59
  100.0 2.0 %collective-permute-start.2 = (bf16[3,128,1536]{2,1,0:T(8,128)(2,1)}, bf16[3,128,1536]{2,1,0:T(8,128)(2,1)}, u32[]{:S(2)}, u32[]{:S(2)}) collective-permute-start(bf16[3,128,1536]{2,1,0:T(8,128)(2,1)} %pad.59), channel_id=1, source_target_pairs={{0,1},{1,2},{2,3},{3,4},{4,5},{5,6},{6,7},{7,8},{8,9},{9,10},{10,1... | collective-permute-start | bytes 3538952 | tf_op jit(solution)/shard_map/ppermute | solution.py:129
  102.1 1.1 pad.60
  103.2 10.2 %collective-permute-start.3 = (bf16[3,128,1536]{2,1,0:T(8,128)(2,1)}, bf16[3,128,1536]{2,1,0:T(8,128)(2,1)}, u32[]{:S(2)}, u32[]{:S(2)}) collective-permute-start(bf16[3,128,1536]{2,1,0:T(8,128)(2,1)} %pad.60), channel_id=1, source_target_pairs={{1,0},{2,1},{3,2},{4,3},{5,4},{6,5},{7,6},{8,7},{9,8},{10,9},{11,1... | collective-permute-start | bytes 3538952 | tf_op jit(solution)/shard_map/ppermute | solution.py:129
  113.5 12.8 %tap_grads.1 = f32[8,1,1120]{2,1,0:T(1,128)S(1)} custom-call(bf16[3,128,1536]{2,1,0:T(8,128)(2,1)S(1)} %collective-permute-done.above, bf16[4,128,1440]{2,1,0:T(8,128)(2,1)S(1)} %bitcast.71, bf16[3,128,1536]{2,1,0:T(8,128)(2,1)S(1)} %collective-permute-done.1.below, bf16[4,128,1440]{2,1,0:T(8,128)(2,1)S(1)} %get-tuple-element.18.own.grads), custom_call_target="tpu_custom_call" | custom-call | flops 16515072000 | bytes 8847360 | tf_op jit(solution)/shard_map/tap_grads/pallas_call | solution.py:212
  126.8 0.1 reshape.129
  127.1 0.1 reshape.130
  127.4 0.8 pad_maximum_fusion
  128.2 6.0 %all-to-all-start.2 = ((f32[16,45,128]{2,1,0:T(8,128)}), f32[16,45,128]{2,1,0:T(8,128)S(1)}, u32[]{:S(2)}, u32[]{:S(2)}) async-start(f32[16,45,128]{2,1,0:T(8,128)} %pad_maximum_fusion), calls=%async_computation.2 | async-start | bytes 786432 | tf_op jit(solution)/shard_map/all_to_all | solution.py:233
  134.3 12.6 %depthwise_back.1 = bf16[4,128,1440]{2,1,0:T(8,128)(2,1)S(1)} custom-call(bf16[3,128,1536]{2,1,0:T(8,128)(2,1)} %collective-permute-done.2.above, bf16[4,128,1440]{2,1,0:T(8,128)(2,1)} %copy-done.2, bf16[3,128,1536]{2,1,0:T(8,128)(2,1)} %collective-permute-done.3.below, bf16[4,128,1440]{2,1,0:T(8,128)(2,1)} %bitcast.79, bf16[4,128,1120]{2,1,0:T(8,128)(2,1)S(1)} %copy-done.3), custom_call_target="tpu_custom_call" | custom-call | flops 16515072000 | bytes 8847360 | tf_op jit(solution)/shard_map/depthwise_back/pallas_call | solution.py:236
  146.9 2.4 %copy.105 = bf16[1,128,4,1440]{3,2,0,1:T(4,128)(2,1)} copy(bf16[1,128,4,1440]{3,1,2,0:T(8,128)(2,1)S(1)} %bitcast.73) | data formatting | bytes 2949120 | tf_op jit(solution)/shard_map/broadcast_in_dim | solution.py:249
  149.2 10.8 %all-to-all-start.1 = ((bf16[1,128,4,1440]{3,2,0,1:T(4,128)(2,1)}), bf16[1,128,4,1440]{3,2,0,1:T(4,128)(2,1)S(1)}, u32[]{:S(2)}, u32[]{:S(2)}) async-start(bf16[1,128,4,1440]{3,2,0,1:T(4,128)(2,1)} %copy.105), calls=%async_computation.1 | async-start | bytes 3145728 | tf_op jit(solution)/shard_map/all_to_all | solution.py:248
  160.0 1.5 copy.109
  161.7 0.6 copy.110
  162.3 0.6 reshape.132
  162.9 0.6 reshape.133
  163.5 0.6 slice_bitcast_fusion.1
  164.1 0.5 slice_bitcast_fusion.2
  164.6 31.6 %all-to-all-done.1 = bf16[1,128,4,1440]{3,2,0,1:T(4,128)(2,1)S(1)} async-done(((bf16[1,128,4,1440]{3,2,0,1:T(4,128)(2,1)}), bf16[1,128,4,1440]{3,2,0,1:T(4,128)(2,1)S(1)}, u32[]{:S(2)}, u32[]{:S(2)}) %all-to-all-start.1) | async-done | bytes 1474592 | tf_op jit(solution)/shard_map/all_to_all | solution.py:248
  196.2 0.5 copy.106
  196.7 1.6 all_to_all.33
  (94 shorter events, 1.7 us)
Async XLA Ops:
  4.1 6.7 %copy-start.24 = (f32[128,7,7]{0,2,1:T(8,128)S(1)}, f32[128,7,7]{0,2,1:T(8,128)}, u32[]{:S(2)}) copy-start(f32[128,7,7]{0,2,1:T(8,128)} %param.15) | copy-start | bytes 75268
  4.1 9.3 %copy-start.22 = (bf16[1,128,4,1440]{1,3,2,0:T(8,128)(2,1)S(1)}, bf16[1,128,4,1440]{1,3,2,0:T(8,128)(2,1)}, u32[]{:S(2)}) copy-start(bf16[1,128,4,1440]{1,3,2,0:T(8,128)(2,1)} %param.13) | copy-start | bytes 4423684
  4.1 42.9 %all-to-all-start = ((bf16[1,8,64,1440]{3,1,0,2:T(8,128)(2,1)}), bf16[1,8,64,1440]{3,1,0,2:T(8,128)(2,1)S(1)}, u32[]{:S(2)}, u32[]{:S(2)}) async-start(bf16[1,8,64,1440]{3,1,0,2:T(8,128)(2,1)} %copy.86), calls=%async_computation | async-start | bytes 3145728 | tf_op jit(solution)/shard_map/all_to_all | solution.py:155
  13.3 1.6 copy-start.29
  13.3 1.8 copy-start.4
  13.3 1.9 copy-start.5
  47.1 1.1 copy-start
  48.3 6.0 %copy-start.23 = (bf16[70,1120,1]{1,0,2:T(8,128)(2,1)S(1)}, bf16[70,1120,1]{1,0,2:T(8,128)(2,1)}, u32[]{:S(2)}) copy-start(bf16[70,1120,1]{1,0,2:T(8,128)(2,1)} %constant.72) | copy-start | bytes 470404
  48.3 6.0 %copy-start.25 = (bf16[1,128,70]{1,2,0:T(8,128)(2,1)S(1)}, bf16[1,128,70]{1,2,0:T(8,128)(2,1)}, u32[]{:S(2)}) copy-start(bf16[1,128,70]{1,2,0:T(8,128)(2,1)} %stack.30) | copy-start | bytes 53764
  48.3 6.0 %copy-start.26 = (bf16[1,128,70]{1,2,0:T(8,128)(2,1)S(1)}, bf16[1,128,70]{1,2,0:T(8,128)(2,1)}, u32[]{:S(2)}) copy-start(bf16[1,128,70]{1,2,0:T(8,128)(2,1)} %stack.31) | copy-start | bytes 53764
  48.4 6.0 %copy-start.27 = (bf16[1,128,70]{1,2,0:T(8,128)(2,1)S(1)}, bf16[1,128,70]{1,2,0:T(8,128)(2,1)}, u32[]{:S(2)}) copy-start(bf16[1,128,70]{1,2,0:T(8,128)(2,1)} %stack.32) | copy-start | bytes 53764
  48.4 6.0 %copy-start.28 = (bf16[1,128,70]{1,2,0:T(8,128)(2,1)S(1)}, bf16[1,128,70]{1,2,0:T(8,128)(2,1)}, u32[]{:S(2)}) copy-start(bf16[1,128,70]{1,2,0:T(8,128)(2,1)} %stack.33) | copy-start | bytes 53764
  48.4 16.9 %collective-permute-start = (bf16[3,128,1536]{2,1,0:T(8,128)(2,1)S(1)}, bf16[3,128,1536]{2,1,0:T(8,128)(2,1)S(1)}, u32[]{:S(2)}, u32[]{:S(2)}) collective-permute-start(bf16[3,128,1536]{2,1,0:T(8,128)(2,1)S(1)} %pad.53), channel_id=1, source_target_pairs={{0,1},{1,2},{2,3},{3,4},{4,5},{5,6},{6,7},{7,8},{8,9},{9,10},{10,1... | collective-permute-start | bytes 3538952 | tf_op jit(solution)/shard_map/ppermute | solution.py:129
  52.2 18.5 %collective-permute-start.1 = (bf16[3,128,1536]{2,1,0:T(8,128)(2,1)S(1)}, bf16[3,128,1536]{2,1,0:T(8,128)(2,1)S(1)}, u32[]{:S(2)}, u32[]{:S(2)}) collective-permute-start(bf16[3,128,1536]{2,1,0:T(8,128)(2,1)S(1)} %pad.54), channel_id=1, source_target_pairs={{1,0},{2,1},{3,2},{4,3},{5,4},{6,5},{7,6},{8,7},{9,8},{10,9},{11,1... | collective-permute-start | bytes 3538952 | tf_op jit(solution)/shard_map/ppermute | solution.py:129
  56.4 26.6 %copy-start.6 = (f32[128,1]{1,0:T(8,128)S(1)}, f32[128,1]{1,0:T(8,128)}, u32[]{:S(2)}) copy-start(f32[128,1]{1,0:T(8,128)} %copy.96.gain) | copy-start | bytes 1540
  56.4 26.7 %copy-start.7 = (f32[128,1]{1,0:T(8,128)S(1)}, f32[128,1]{1,0:T(8,128)}, u32[]{:S(2)}) copy-start(f32[128,1]{1,0:T(8,128)} %copy.97.shift) | copy-start | bytes 1540
  56.4 26.7 %copy-start.8 = (f32[128,1]{1,0:T(8,128)S(1)}, f32[128,1]{1,0:T(8,128)}, u32[]{:S(2)}) copy-start(f32[128,1]{1,0:T(8,128)} %copy.99.out_off) | copy-start | bytes 1540
  56.4 26.7 %copy-start.15 = (s32[4,1,1440]{2,1,0:T(1,128)S(1)}, s32[4,1,1440]{2,1,0:T(1,128)}, u32[]{:S(2)}) copy-start(s32[4,1,1440]{2,1,0:T(1,128)} %broadcast_in_dim.55.mask) | copy-start | bytes 69124
  98.1 0.7 copy-start.9
  98.1 0.7 copy-start.11
  98.1 0.8 copy-start.13
  98.1 0.8 copy-start.16
  98.1 0.8 copy-start.18
  98.1 0.8 copy-start.20
  98.1 15.3 %copy-start.2 = (bf16[4,128,1440]{2,1,0:T(8,128)(2,1)}, bf16[4,128,1440]{2,1,0:T(8,128)(2,1)S(1)}, u32[]{:S(2)}) copy-start(bf16[4,128,1440]{2,1,0:T(8,128)(2,1)S(1)} %get-tuple-element.18.own.grads) | copy-start | bytes 4423684
  100.0 13.4 %copy-start.1 = (bf16[1,8,16,4,1440]{4,1,2,3,0:T(8,128)(2,1)S(1)}, bf16[1,8,16,4,1440]{4,1,2,3,0:T(8,128)(2,1)}, u32[]{:S(2)}) copy-start(bf16[1,8,16,4,1440]{4,1,2,3,0:T(8,128)(2,1)} %copy-done) | copy-start | bytes 4423684
  100.0 34.2 %collective-permute-start.2 = (bf16[3,128,1536]{2,1,0:T(8,128)(2,1)}, bf16[3,128,1536]{2,1,0:T(8,128)(2,1)}, u32[]{:S(2)}, u32[]{:S(2)}) collective-permute-start(bf16[3,128,1536]{2,1,0:T(8,128)(2,1)} %pad.59), channel_id=1, source_target_pairs={{0,1},{1,2},{2,3},{3,4},{4,5},{5,6},{6,7},{7,8},{8,9},{9,10},{10,1... | collective-permute-start | bytes 3538952 | tf_op jit(solution)/shard_map/ppermute | solution.py:129
  103.2 23.1 %copy-start.14 = (f32[256,1]{1,0:T(8,128)S(1)}, f32[256,1]{1,0:T(8,128)}, u32[]{:S(2)}) copy-start(f32[256,1]{1,0:T(8,128)} %copy-done.13) | copy-start | bytes 3076
  103.2 23.2 %copy-start.21 = (f32[128,1]{1,0:T(8,128)S(1)}, f32[128,1]{1,0:T(8,128)}, u32[]{:S(2)}) copy-start(f32[128,1]{1,0:T(8,128)} %copy-done.20) | copy-start | bytes 1540
  103.2 23.3 %copy-start.19 = (f32[128,1]{1,0:T(8,128)S(1)}, f32[128,1]{1,0:T(8,128)}, u32[]{:S(2)}) copy-start(f32[128,1]{1,0:T(8,128)} %copy-done.18) | copy-start | bytes 1540
  103.2 23.4 %copy-start.17 = (f32[128,1]{1,0:T(8,128)S(1)}, f32[128,1]{1,0:T(8,128)}, u32[]{:S(2)}) copy-start(f32[128,1]{1,0:T(8,128)} %copy-done.16) | copy-start | bytes 1540
  103.2 31.0 %collective-permute-start.3 = (bf16[3,128,1536]{2,1,0:T(8,128)(2,1)}, bf16[3,128,1536]{2,1,0:T(8,128)(2,1)}, u32[]{:S(2)}, u32[]{:S(2)}) collective-permute-start(bf16[3,128,1536]{2,1,0:T(8,128)(2,1)} %pad.60), channel_id=1, source_target_pairs={{1,0},{2,1},{3,2},{4,3},{5,4},{6,5},{7,6},{8,7},{9,8},{10,9},{11,1... | collective-permute-start | bytes 3538952 | tf_op jit(solution)/shard_map/ppermute | solution.py:129
  126.2 1.1 copy-start.12
  126.3 1.1 copy-start.10
  127.0 7.2 %copy-start.3 = (bf16[4,128,1120]{2,1,0:T(8,128)(2,1)S(1)}, bf16[4,128,1120]{2,1,0:T(8,128)(2,1)}, u32[]{:S(2)}) copy-start(bf16[4,128,1120]{2,1,0:T(8,128)(2,1)} %fusion.1.band) | copy-start | bytes 3440644
  128.2 21.0 %all-to-all-start.2 = ((f32[16,45,128]{2,1,0:T(8,128)}), f32[16,45,128]{2,1,0:T(8,128)S(1)}, u32[]{:S(2)}, u32[]{:S(2)}) async-start(f32[16,45,128]{2,1,0:T(8,128)} %pad_maximum_fusion), calls=%async_computation.2 | async-start | bytes 786432 | tf_op jit(solution)/shard_map/all_to_all | solution.py:233
  149.2 46.9 %all-to-all-start.1 = ((bf16[1,128,4,1440]{3,2,0,1:T(4,128)(2,1)}), bf16[1,128,4,1440]{3,2,0,1:T(4,128)(2,1)S(1)}, u32[]{:S(2)}, u32[]{:S(2)}) async-start(bf16[1,128,4,1440]{3,2,0,1:T(4,128)(2,1)} %copy.105), calls=%async_computation.1 | async-start | bytes 3145728 | tf_op jit(solution)/shard_map/all_to_all | solution.py:248
